TPU v7x, 32 devices: a whole 2x2x4 slice. The times are simulated.
32 devices in a mesh: groups: 2 (over y), gz: 4 (over z), view: 2 (over x), gy: 2 (over core).
Axes of the slice: x: 2, y: 2, z: 4, core: 2. Of those that a mesh axis runs over, the one named last changes fastest.
Arguments:
- camera: float32 [2, 256, 3, 128, 128], P('view', ('groups', 'gz'), None, 'gy'), parts along dimension 1, may hold values from 0 to 4
- background: int32 [2, 2, 8], P('view', 'gy', ('groups', 'gz')), parts along dimension 2, may hold values from 0 to 2
- destination: int32 [2, 2, 256, 1], P('view', 'gy', ('groups', 'gz')), parts along dimension 2, may hold values from 0 to 3; in each aligned block of 32 rows (0 to 31, 32 to 63, ..., all dimensions but the last counted through in order) at most 16 rows name the same one
- offsets: int32 [2, 2, 256], P('view', 'gy', ('groups', 'gz')), parts along dimension 2, may hold values from 0 to 6
- shift_frac: float32 [2, 3], P('view'), may hold values from 0.15 to 0.85
- psf_taps: float32 [2, 3, 9], P('view'), may hold values from 0.05 to 1
Outputs:
- estimate: float32 [64, 128, 128], P(('groups', 'gz'), 'gy'), parts along dimension 0
- joined_views: float32 [2, 64, 128, 128], P('view', ('groups', 'gz'), 'gy'), parts along dimension 1
There are 2 independent parts, one for each index of `groups`. A program takes and returns all parts, laid end to end along the dimension named above; an argument that names none is the same for every part. Nothing has to cross between parts.
Inputs may be any that keep to these rules, and one draw needn't show every extreme that they name: `destination`: within the 32 block rows of one tile, no slab is named more than 16 times; some tile names one slab exactly 16 times.
All inputs are finite; a program needn't handle non-finite values.
Results may differ from a plain program's by a relative error of at most 0.0001.
Values sent between devices are 32-bit elements; how exact they have to be, the bound alone decides.
A program may use at most 64 MiB of HBM per device.

v0:
```python
import functools

import jax
import jax.numpy as jnp
from jax import lax
from jax.experimental import pallas as pl
from jax.experimental.pallas import tpu as pltpu
from jax.sharding import PartitionSpec as P

CZ = 8
ITERS = 2
HALO = 8
CHUNK = 4

DATA_FLOOR = 0.25
MESH = pl.DeviceIdType.MESH


def deposit_kernel(rows, dest, offs, level, frac, psf, cam_ref, acc_ref, tap_ref, cam, sems):
    taps = psf.shape[2]
    blocks, planes = cam_ref.shape[:2]

    def fetch(c):
        at = pl.ds(c * CHUNK, CHUNK)
        return pltpu.make_async_copy(cam_ref.at[at], cam.at[at], sems.at[c])

    for c in range(blocks // CHUNK):
        fetch(c).start()

    @pl.loop(0, acc_ref.shape[0])
    def _(s):
        acc_ref[s] = jnp.zeros(acc_ref.shape[1:], jnp.float32)

    tap_ref[...] = jnp.zeros(tap_ref.shape, jnp.float32)
    for axis in range(3):
        scale = jnp.sum(psf[axis], axis=1, keepdims=True)
        share = psf[axis] / scale
        for t in range(taps):
            at = axis * taps + t
            tap_ref[at : at + 1, :] = jnp.broadcast_to(share[:, t : t + 1], (1, 128))

    fz = frac[0]
    base = level[0].astype(jnp.float32)

    @pl.loop(0, blocks // CHUNK)
    def _(c):
        fetch(c).wait()
        for i in range(CHUNK):
            b = c * CHUNK + i
            s = dest[b]
            o = offs[b]
            lower = cam[b, 0] - base
            for k in range(planes - 1):
                upper = cam[b, k + 1] - base
                at = pl.ds(pl.multiple_of((o + k) * rows, 8), rows)
                acc_ref[s, at, :] = acc_ref[s, at, :] + ((1.0 - fz) * lower + fz * upper)
                cnt = pl.ds(CZ * rows + o + k, 1)
                acc_ref[s, cnt, :] = acc_ref[s, cnt, :] + 1.0
                lower = upper


def world_kernel(
    dims, rows, taps,
    frac, acc_ref, tap_in, est_ref, joined_ref,
    recv, tap_all, jx, e0, e1, kx, za, zb, rt, yb, lg,
    a2a_s, a2a_r, own_sem, tap_s, tap_r, row_s, row_r, lo_s, lo_r, hi_s, hi_r, loc_sem,
    zs, zr, es, er, out_s, out_r,
):
    slabs, views, bands = dims
    strip = rows // views
    wide = strip + 2 * HALO
    margin = taps // 2
    z = lax.axis_index("gz")
    v = lax.axis_index("view")
    g = lax.axis_index("gy")

    def snake(band, place):
        return jnp.where(band % 2 == 1, views - 1 - place, place)

    idx = snake(g, v)
    me = g * views + idx
    strips = views * bands

    def dev(zz, vv, gg):
        return {"gz": zz, "view": vv, "gy": gg}

    def strip_dev(zz, ss):
        band = ss // views
        return dev(zz, snake(band, ss % views), band)

    below, above = z > 0, z < slabs - 1
    left, right = me > 0, me < strips - 1

    @pl.loop(0, views)
    def _(w):
        @pl.loop(0, 3 * CZ)
        def _(p):
            jx[w, p] = jnp.zeros((wide, 128), jnp.float32)

    @pl.loop(0, 3 * CZ)
    def _(p):
        e1[p] = jnp.zeros((wide, 128), jnp.float32)

    barrier = pltpu.get_barrier_semaphore()

    def greet(target):
        pl.semaphore_signal(barrier, inc=1, device_id=target, device_id_type=MESH)

    for d in range(1, slabs):
        greet(dev((z + d) % slabs, v, g))
    for d in range(1, strips):
        greet(strip_dev(z, (me + d) % strips))
    corners = []
    for dz, zok in ((-1, below), (1, above)):
        for ds, sok in ((-1, left), (1, right)):
            corners.append((dz, ds, zok & sok))
    amount = slabs - 1 + strips - 1
    for dz, ds, ok in corners:
        amount = amount + ok.astype(jnp.int32)

        @pl.when(ok)
        def _(dz=dz, ds=ds):
            greet(strip_dev(z + dz, me + ds))

    pl.semaphore_wait(barrier, amount)

    def a2a(d):
        to = (z + d) % slabs
        return pltpu.make_async_remote_copy(
            src_ref=acc_ref.at[to], dst_ref=recv.at[d - 1], send_sem=a2a_s.at[d - 1],
            recv_sem=a2a_r.at[d - 1], device_id=dev(to, v, g), device_id_type=MESH)

    for d in range(1, slabs):
        a2a(d).start()
    own = pltpu.make_async_copy(acc_ref.at[z], recv.at[slabs - 1], own_sem)
    own.start()
    own_tap = pltpu.make_async_copy(tap_in, tap_all.at[v], loc_sem.at[1])
    own_tap.start()

    def tap_copy(d):
        return pltpu.make_async_remote_copy(
            src_ref=tap_in, dst_ref=tap_all.at[v], send_sem=tap_s.at[d - 1],
            recv_sem=tap_r.at[d - 1], device_id={"view": (v + d) % views}, device_id_type=MESH)

    for d in range(1, views):
        tap_copy(d).start()
    own_tap.wait()
    for d in range(1, views):
        tap_copy(d).wait()

    apart = lax.broadcasted_iota(jnp.int32, (128, 128), 0) - lax.broadcasted_iota(jnp.int32, (128, 128), 1)

    @pl.loop(0, views)
    def _(w):
        ahead = jnp.zeros((128, 128), jnp.float32)
        back = jnp.zeros((128, 128), jnp.float32)
        for t in range(taps):
            tap = tap_all[w, 2 * taps + t : 2 * taps + t + 1, :]
            ahead = jnp.where(apart == t - margin, tap, ahead)
            back = jnp.where(apart == margin - t, tap, back)
        for n, full in enumerate((ahead, back)):
            top = full.astype(jnp.bfloat16)
            kx[w, n, 0:128, 0:128] = top
            kx[w, n, 128:256, 0:128] = top
            kx[w, n, 0:128, 128:256] = (full - top.astype(jnp.float32)).astype(jnp.bfloat16)
            kx[w, n, 128:256, 128:256] = jnp.zeros((128, 128), jnp.bfloat16)

    own.wait()
    for d in range(1, slabs):
        a2a(d).wait_recv()

    fy, fx = frac[1], frac[2]
    last_row = lax.broadcasted_iota(jnp.int32, (rows, 128), 0) == rows - 1
    last_col = lax.broadcasted_iota(jnp.int32, (rows, 128), 1) == 127

    @pl.loop(0, CZ)
    def _(p):
        at = pl.ds(pl.multiple_of(p * rows, 8), rows)
        cnt = pl.ds(CZ * rows + p, 1)
        total = recv[0, at, :]
        covered = recv[0, cnt, :]
        for s in range(1, slabs):
            total = total + recv[s, at, :]
            covered = covered + recv[s, cnt, :]
        follow = jnp.where(last_row, total, pltpu.roll(total, rows - 1, 0))
        total = (1.0 - fy) * total + fy * follow
        follow = jnp.where(last_col, total, pltpu.roll(total, 127, 1))
        total = (1.0 - fx) * total + fx * follow
        joined_ref[0, p] = jnp.maximum(total / (covered + 1.0), DATA_FLOOR)

    joined = joined_ref.at[0]
    mid = pl.ds(CZ, CZ)

    def main_piece(i):
        lo, hi = max(i * strip - HALO, 0), min((i + 1) * strip + HALO, rows)
        return pl.ds(lo, hi - lo), pl.ds(lo - i * strip + HALO, hi - lo)

    def main_copy(i, target, sem_at):
        src, dst = main_piece(i)
        return pltpu.make_async_remote_copy(
            src_ref=joined.at[:, src, :], dst_ref=jx.at[v, mid, dst, :], send_sem=row_s.at[i],
            recv_sem=row_r.at[sem_at], device_id={"view": target}, device_id_type=MESH)

    def main_local(i):
        src, dst = main_piece(i)
        return pltpu.make_async_copy(joined.at[:, src, :], jx.at[v, mid, dst, :], loc_sem.at[0])

    def edge_copy(up):
        src = pl.ds(rows - HALO, HALO) if up else pl.ds(0, HALO)
        dst = pl.ds(0, HALO) if up else pl.ds(HALO + strip, HALO)
        sems = (lo_s, lo_r) if up else (hi_s, hi_r)
        target = strip_dev(z, (g + 1) * views if up else g * views - 1)
        return pltpu.make_async_remote_copy(
            src_ref=joined.at[:, src, :], dst_ref=jx.at[v, mid, dst, :], send_sem=sems[0],
            recv_sem=sems[1].at[v], device_id=target, device_id_type=MESH)

    for i in range(views):
        owner = snake(g, i)

        @pl.when(owner != v)
        def _(i=i, owner=owner):
            main_copy(i, owner, v).start()

        @pl.when(owner == v)
        def _(i=i):
            main_local(i).start()

    next_band, prev_band = g < bands - 1, g > 0

    @pl.when(next_band)
    def _():
        edge_copy(True).start()

    @pl.when(prev_band)
    def _():
        edge_copy(False).start()

    def z_copy(w, up):
        dst = pl.ds(0, CZ) if up else pl.ds(2 * CZ, CZ)
        side = 1 if up else 0
        return pltpu.make_async_remote_copy(
            src_ref=jx.at[w, mid], dst_ref=jx.at[w, dst], send_sem=zs.at[side, w],
            recv_sem=zr.at[side, w], device_id={"gz": z + 1 if up else z - 1}, device_id_type=MESH)

    for d in range(views):
        w = (v + d) % views
        for i in range(views):
            if d == 0:
                @pl.when(idx == i)
                def _(i=i):
                    main_local(i).wait()
            else:
                @pl.when(idx == i)
                def _(i=i, w=w):
                    main_copy(i, v, w).wait_recv()

        @pl.when((idx == 0) & prev_band)
        def _(w=w):
            pltpu.make_async_remote_copy(
                src_ref=joined.at[:, pl.ds(rows - HALO, HALO), :], dst_ref=jx.at[w, mid, pl.ds(0, HALO), :],
                send_sem=lo_s, recv_sem=lo_r.at[w], device_id={"view": v}, device_id_type=MESH).wait_recv()

        @pl.when((idx == views - 1) & next_band)
        def _(w=w):
            pltpu.make_async_remote_copy(
                src_ref=joined.at[:, pl.ds(0, HALO), :], dst_ref=jx.at[w, mid, pl.ds(HALO + strip, HALO), :],
                send_sem=hi_s, recv_sem=hi_r.at[w], device_id={"view": v}, device_id_type=MESH).wait_recv()

        @pl.when(above)
        def _(w=w):
            z_copy(w, True).start()

        @pl.when(below)
        def _(w=w):
            z_copy(w, False).start()

    for d in range(views):
        w = (v + d) % views

        @pl.when(below)
        def _(w=w):
            z_copy(w, True).wait_recv()

        @pl.when(above)
        def _(w=w):
            z_copy(w, False).wait_recv()

    @pl.loop(0, 3 * CZ)
    def _(p):
        total = jx[0, p]
        for w in range(1, views):
            total = total + jx[w, p]
        e0[p] = total / views

    planes_r = CZ + 2 * margin
    rows_r = strip + 2 * margin

    def along_x(u, w, n):
        top = u.astype(jnp.bfloat16)
        rest = (u - top.astype(jnp.float32)).astype(jnp.bfloat16)
        both = jnp.dot(jnp.concatenate([top, rest], axis=1), kx[w, n], preferred_element_type=jnp.float32)
        return both[:, 0:128] + both[:, 128:256]

    def weighted(terms, weights):
        total = weights[0] * terms[0]
        for term, weight in zip(terms[1:], weights[1:]):
            total = total + weight * term
        return total

    def correct(est):
        for w in range(views):
            def tap(axis, t):
                at = axis * taps + t
                return tap_all[w, at : at + 1, :]

            @pl.loop(0, wide // 8, unroll=2)
            def _(r):
                at = pl.ds(pl.multiple_of(r * 8, 8), 8)
                column = [est[CZ - 2 * margin + p, at, :] for p in range(planes_r + 2 * margin)]
                for p in range(planes_r):
                    za[p, at, :] = weighted(column[p : p + taps], [tap(0, t) for t in range(taps)])

            @pl.loop(0, planes_r, unroll=4)
            def _(p):
                base = HALO - 2 * margin
                zb[p] = weighted([za[p, base + t : base + t + rows_r, :] for t in range(taps)],
                                 [tap(1, t) for t in range(taps)])

            @pl.loop(0, planes_r // 4)
            def _(c):
                at = pl.ds(c * 4, 4)
                blurred = along_x(zb[at].reshape(4 * rows_r, 128), w, 0).reshape(4, rows_r, 128)
                data = jx[w, pl.ds(c * 4 + CZ - margin, 4), HALO - margin : HALO - margin + rows_r, :]
                rt[at] = jnp.where(data > 0.0, data / blurred, 0.0)

            @pl.loop(0, rows_r // 8, unroll=True)
            def _(r):
                at = pl.ds(pl.multiple_of(r * 8, 8), 8)
                column = [rt[p, at, :] for p in range(planes_r)]
                for p in range(CZ):
                    za[p, at, :] = weighted(column[p : p + taps], [tap(0, taps - 1 - t) for t in range(taps)])

            @pl.loop(0, CZ, unroll=4)
            def _(p):
                yb[p] = weighted([za[p, t : t + strip, :] for t in range(taps)],
                                 [tap(1, taps - 1 - t) for t in range(taps)])

            @pl.loop(0, CZ // 4)
            def _(c):
                at = pl.ds(c * 4, 4)
                logs = jnp.log(along_x(yb[at].reshape(4 * strip, 128), w, 1)).reshape(4, strip, 128)
                lg[at] = logs if w == 0 else lg[at] + logs

    inner = pl.ds(HALO, strip)
    near = []
    for n, (dz, ds) in enumerate([(a, b) for a in (-1, 0, 1) for b in (-1, 0, 1) if a or b]):
        zok = {-1: below, 0: z >= 0, 1: above}[dz]
        sok = {-1: left, 0: z >= 0, 1: right}[ds]
        far_z = {-1: above, 0: z >= 0, 1: below}[dz]
        far_s = {-1: right, 0: z >= 0, 1: left}[ds]
        near.append((n, dz, ds, zok & sok, far_z & far_s))

    def near_copy(n, dz, ds):
        src_r = {-1: pl.ds(HALO, HALO), 0: inner, 1: pl.ds(strip, HALO)}[ds]
        dst_r = {-1: pl.ds(HALO + strip, HALO), 0: inner, 1: pl.ds(0, HALO)}[ds]
        dst_p = {-1: pl.ds(2 * CZ, CZ), 0: mid, 1: pl.ds(0, CZ)}[dz]
        return pltpu.make_async_remote_copy(
            src_ref=e1.at[mid, src_r, :], dst_ref=e1.at[dst_p, dst_r, :], send_sem=es.at[n],
            recv_sem=er.at[n], device_id=strip_dev(z + dz, me + ds), device_id_type=MESH)

    def out_copy(target, sem_at):
        at = pl.ds(pl.multiple_of(idx * strip, 8), strip)
        return pltpu.make_async_remote_copy(
            src_ref=lg, dst_ref=est_ref.at[:, at, :], send_sem=out_s.at[sem_at],
            recv_sem=out_r.at[sem_at], device_id={"view": target}, device_id_type=MESH)

    correct(e0)
    for p in range(CZ):
        e1[CZ + p, inner, :] = e0[CZ + p, inner, :] * jnp.exp(lg[p] / views)
    for n, dz, ds, ok, _ in near:
        @pl.when(ok)
        def _(n=n, dz=dz, ds=ds):
            near_copy(n, dz, ds).start()
    for n, dz, ds, _, ok in near:
        @pl.when(ok)
        def _(n=n, dz=dz, ds=ds):
            near_copy(n, dz, ds).wait_recv()

    correct(e1)
    mine = pl.ds(pl.multiple_of(idx * strip, 8), strip)
    for p in range(CZ):
        done = e1[CZ + p, inner, :] * jnp.exp(lg[p] / views)
        lg[p] = done
        est_ref[p, mine, :] = done
    for d in range(1, views):
        out_copy((v + d) % views, d - 1).start()
    for d in range(1, views):
        out_copy((v + d) % views, d - 1).wait()

    for d in range(1, slabs):
        a2a(d).wait_send()
    for i in range(views):
        owner = snake(g, i)

        @pl.when(owner != v)
        def _(i=i, owner=owner):
            main_copy(i, owner, v).wait_send()

    @pl.when(next_band)
    def _():
        edge_copy(True).wait_send()

    @pl.when(prev_band)
    def _():
        edge_copy(False).wait_send()

    for w in range(views):
        @pl.when(above)
        def _(w=w):
            z_copy(w, True).wait_send()

        @pl.when(below)
        def _(w=w):
            z_copy(w, False).wait_send()

    for n, dz, ds, ok, _ in near:
        @pl.when(ok)
        def _(n=n, dz=dz, ds=ds):
            near_copy(n, dz, ds).wait_send()


def on_device(dims, camera, background, destination, offsets, shift_frac, psf_taps):
    slabs, views, bands = dims
    blocks, planes, rows, cols = camera.shape[1:]
    taps = psf_taps.shape[-1]
    margin = taps // 2
    tall = CZ * rows + CZ
    strip = rows // views
    wide = strip + 2 * HALO
    tap_rows = -(-3 * taps // 8) * 8
    smem = pl.BlockSpec(memory_space=pltpu.SMEM)
    vmem = pl.BlockSpec(memory_space=pltpu.VMEM)
    acc, tap_rows_all = pl.pallas_call(
        functools.partial(deposit_kernel, rows),
        in_specs=[smem] * 4 + [vmem, pl.BlockSpec(memory_space=pl.ANY)],
        out_specs=(vmem, vmem),
        out_shape=(
            jax.ShapeDtypeStruct((slabs, tall, cols), jnp.float32),
            jax.ShapeDtypeStruct((tap_rows, cols), jnp.float32),
        ),
        scratch_shapes=[
            pltpu.VMEM((blocks, planes, rows, cols), jnp.float32),
            pltpu.SemaphoreType.DMA((blocks // CHUNK,)),
        ],
        compiler_params=pltpu.CompilerParams(vmem_limit_bytes=60 * 1024 * 1024),
        name="deposit",
    )(destination.reshape(-1), offsets.reshape(-1), background.reshape(-1), shift_frac[0], jnp.transpose(psf_taps, (1, 0, 2)), camera[0])

    dma = pltpu.SemaphoreType.DMA
    f32 = jnp.float32
    estimate, joined = pl.pallas_call(
        functools.partial(world_kernel, dims, rows, taps),
        in_specs=[smem, vmem, vmem],
        out_specs=(vmem, vmem),
        out_shape=(
            jax.ShapeDtypeStruct((CZ, rows, cols), f32),
            jax.ShapeDtypeStruct((1, CZ, rows, cols), f32),
        ),
        scratch_shapes=[
            pltpu.VMEM((slabs, tall, cols), f32),
            pltpu.VMEM((views, tap_rows, cols), f32),
            pltpu.VMEM((views, 3 * CZ, wide, cols), f32),
            pltpu.VMEM((3 * CZ, wide, cols), f32),
            pltpu.VMEM((3 * CZ, wide, cols), f32),
            pltpu.VMEM((views, 2, 2 * cols, 2 * cols), jnp.bfloat16),
            pltpu.VMEM((CZ + 2 * margin, wide, cols), f32),
            pltpu.VMEM((CZ + 2 * margin, strip + 2 * margin, cols), f32),
            pltpu.VMEM((CZ + 2 * margin, strip + 2 * margin, cols), f32),
            pltpu.VMEM((CZ, strip, cols), f32),
            pltpu.VMEM((CZ, strip, cols), f32),
            dma((slabs,)), dma((slabs,)), dma, dma((views,)), dma((views,)),
            dma((views,)), dma((views,)), dma, dma((views,)), dma, dma((views,)), dma((2,)),
            dma((2, views)), dma((2, views)), dma((8,)), dma((8,)), dma((views,)), dma((views,)),
        ],
        compiler_params=pltpu.CompilerParams(
            collective_id=0, has_side_effects=True, vmem_limit_bytes=40 * 1024 * 1024),
        name="world",
    )(shift_frac[0], acc, tap_rows_all)
    return estimate, joined


def solution(mesh):
    dims = (mesh.shape["gz"], mesh.shape["view"], mesh.shape["gy"])
    return jax.shard_map(
        functools.partial(on_device, dims),
        mesh=mesh,
        in_specs=(
            P("view", ("groups", "gz"), None, "gy", None),
            P("view", "gy", ("groups", "gz")),
            P("view", "gy", ("groups", "gz"), None),
            P("view", "gy", ("groups", "gz")),
            P("view", None),
            P("view", None, None),
        ),
        out_specs=(P(("groups", "gz"), "gy", None), P("view", ("groups", "gz"), "gy", None)),
        check_vma=False,
    )
```

profile of v0, /device:TPU:8, one launch (start us, length us, event | category | flops | bytes accessed | tf_op | source)
XLA Modules:
  0.0 67.5 jit_solution(4908452163243005752)
XLA Ops:
  0.6 0.0 copy-start.2
  1.3 3.6 %deposit.1 = (f32[4,520,128]{2,1,0:T(8,128)}, f32[32,128]{1,0:T(8,128)}) custom-call(s32[32]{0:T(128)} %bitcast.11, s32[32]{0:T(128)} %bitcast.12, s32[1]{0:T(128)} %bitcast.6.level, f32[3]{0:T(128)} %bitcast.7, f32[3,1,9]{2,1,0:T(1,128)} %bitcast.10, f32[32,3,64,128]{3,2,1,0:T(8,128)} %bitcast.9), custom_call_target="tpu_custom_call" | custom-call | tf_op jit(solution)/shard_map/deposit/pallas_call | solution.py:443
  5.0 0.0 copy-done.2
  5.0 0.0 copy-start
  5.0 1.2 %copy-done = f32[4,520,128]{2,1,0:T(8,128)S(1)} copy-done((f32[4,520,128]{2,1,0:T(8,128)S(1)}, f32[4,520,128]{2,1,0:T(8,128)}, u32[]{:S(2)}) %copy-start) | copy-done | bytes 1064984
  6.2 0.0 copy-start.1
  6.2 0.7 %copy-done.1 = f32[32,128]{1,0:T(8,128)S(1)} copy-done((f32[32,128]{1,0:T(8,128)S(1)}, f32[32,128]{1,0:T(8,128)}, u32[]{:S(2)}) %copy-start.1) | copy-done | bytes 16408
  6.9 59.2 %world.1 = (f32[8,64,128]{2,1,0:T(8,128)S(1)}, f32[1,8,64,128]{3,2,1,0:T(8,128)S(1)}) custom-call(f32[3]{0:T(128)S(1)} %bitcast.8, f32[4,520,128]{2,1,0:T(8,128)S(1)} %copy-done, f32[32,128]{1,0:T(8,128)S(1)} %copy-done.1), custom_call_target="tpu_custom_call" | custom-call | tf_op jit(solution)/shard_map/world/pallas_call | solution.py:461
  66.1 0.7 %copy.11 = f32[8,64,128]{2,1,0:T(8,128)} copy(f32[8,64,128]{2,1,0:T(8,128)S(1)} %get-tuple-element.8) | data formatting | bytes 524288
  66.8 0.7 %copy.12 = f32[1,8,64,128]{3,2,1,0:T(8,128)} copy(f32[1,8,64,128]{3,2,1,0:T(8,128)S(1)} %get-tuple-element.9) | data formatting | bytes 524288
Async XLA Ops:
  0.6 4.3 %copy-start.2 = (f32[1,3]{1,0:T(1,128)S(1)}, f32[1,3]{1,0:T(1,128)}, u32[]{:S(2)}) copy-start(f32[1,3]{1,0:T(1,128)} %param.10) | copy-start | bytes 40
  5.0 1.2 %copy-start = (f32[4,520,128]{2,1,0:T(8,128)S(1)}, f32[4,520,128]{2,1,0:T(8,128)}, u32[]{:S(2)}) copy-start(f32[4,520,128]{2,1,0:T(8,128)} %get-tuple-element.4.acc_ref) | copy-start | bytes 3194884
  6.2 0.7 %copy-start.1 = (f32[32,128]{1,0:T(8,128)S(1)}, f32[32,128]{1,0:T(8,128)}, u32[]{:S(2)}) copy-start(f32[32,128]{1,0:T(8,128)} %get-tuple-element.5.tap_in) | copy-start | bytes 49156
where the time goes:
time: 67.8 us; the launch traced here: 67.5 us
  Pallas kernels  62.8 us (93%)
  local copies, waits for them, and re-layouts  3.35 us (5%)
  between operations  1.33 us (2%)
    pallas_call x1, Pallas kernels, on_device(): pl.pallas_call(functools.partial(world_kernel, dims, rows, taps), in_spec...  59.2 us
    pallas_call x1, Pallas kernels, on_device(): pl.pallas_call(functools.partial(deposit_kernel, rows), in_specs=[smem] *...  3.65 us
    unnamed x8, local copies, waits for them, and re-layouts  3.35 us

commit v1 on v0

v1 whole, which is shorter than its diff:
```python
import functools

import jax
import jax.numpy as jnp
from jax import lax
from jax.experimental import pallas as pl
from jax.experimental.pallas import tpu as pltpu
from jax.sharding import PartitionSpec as P

CZ = 8
ITERS = 2
HALO = 8
CHUNK = 4
CP = 2
NCH = CZ // CP
OC = 4
NOUT = CZ // OC

DATA_FLOOR = 0.25
MESH = pl.DeviceIdType.MESH


def deposit_kernel(
    rows, dest_in, offs_in, level_in, frac_in, psf_in, cam_ref, acc_ref, tap_ref,
    dest, offs, level, frac, psf, cam, sems, small,
):
    taps = psf.shape[2]
    blocks, planes = cam_ref.shape[:2]
    pairs = ((dest_in, dest), (offs_in, offs), (level_in, level), (frac_in, frac), (psf_in, psf))
    copies = [pltpu.make_async_copy(a, b, small.at[n]) for n, (a, b) in enumerate(pairs)]
    for copy in copies:
        copy.start()

    def fetch(c):
        at = pl.ds(c * CHUNK, CHUNK)
        return pltpu.make_async_copy(cam_ref.at[at], cam.at[at], sems.at[c])

    for c in range(blocks // CHUNK):
        fetch(c).start()

    @pl.loop(0, acc_ref.shape[0])
    def _(s):
        acc_ref[s] = jnp.zeros(acc_ref.shape[1:], jnp.float32)

    for copy in copies:
        copy.wait()

    tap_ref[...] = jnp.zeros(tap_ref.shape, jnp.float32)
    for axis in range(3):
        scale = jnp.sum(psf[axis], axis=1, keepdims=True)
        share = psf[axis] / scale
        for t in range(taps):
            at = axis * taps + t
            tap_ref[at : at + 1, :] = jnp.broadcast_to(share[:, t : t + 1], (1, 128))
        at = 3 * taps + axis
        tap_ref[at : at + 1, :] = jnp.zeros((1, 128), jnp.float32) + frac[axis]

    fz = frac[0]
    base = level[0, 0, 0].astype(jnp.float32)

    @pl.loop(0, blocks // CHUNK)
    def _(c):
        fetch(c).wait()
        for i in range(CHUNK):
            b = c * CHUNK + i
            s = dest[b]
            o = offs[b]
            lower = cam[b, 0] - base
            for k in range(planes - 1):
                upper = cam[b, k + 1] - base
                at = pl.ds(pl.multiple_of(CZ + (o + k) * rows, 8), rows)
                acc_ref[s, at, :] = acc_ref[s, at, :] + ((1.0 - fz) * lower + fz * upper)
                cnt = pl.ds(o + k, 1)
                acc_ref[s, cnt, :] = acc_ref[s, cnt, :] + 1.0
                lower = upper


def world_kernel(
    dims, rows, taps,
    acc_ref, tap_in, est_ref, joined_ref,
    ru, rd, tap_all, jx, e0, e1, kx, za, zb, rt, yb, lg,
    us, ur, ds_, dr, tap_s, tap_r, loc_sem, ms, mr, los, lor, his, hir,
    zs, zr, es, er, out_s, out_r,
):
    slabs, views, bands = dims
    strip = rows // views
    wide = strip + 2 * HALO
    margin = taps // 2
    z = lax.axis_index("gz")
    v = lax.axis_index("view")
    g = lax.axis_index("gy")
    strips = views * bands
    me = v * bands + g
    band, idx = me // views, me % views

    def dev(zz, vv, gg):
        return {"gz": zz, "view": vv, "gy": gg}

    def strip_dev(zz, ss):
        return dev(zz, ss // bands, ss % bands)

    below, above = z > 0, z < slabs - 1
    left, right = me > 0, me < strips - 1

    barrier = pltpu.get_barrier_semaphore()

    def greet(target):
        pl.semaphore_signal(barrier, inc=1, device_id=target, device_id_type=MESH)

    amount = strips - 1
    for dz, zok in ((-1, below), (1, above)):
        for ds, sok in ((-1, left), (0, z >= 0), (1, right)):
            ok = zok & sok
            amount = amount + ok.astype(jnp.int32)

            @pl.when(ok)
            def _(dz=dz, ds=ds):
                greet(strip_dev(z + dz, me + ds))

    for d in range(1, strips):
        greet(strip_dev(z, (me + d) % strips))

    def clear(ref, planes, lo, hi):
        @pl.loop(planes[0], planes[1])
        def _(p):
            ref[p, lo:hi, :] = jnp.zeros((hi - lo, 128), jnp.float32)

    for edge, flow, halo in ((z == 0, ru, (0, CZ)), (z == slabs - 1, rd, (2 * CZ, 3 * CZ))):
        @pl.when(edge)
        def _(flow=flow, halo=halo):
            flow[z] = jnp.zeros(flow.shape[1:], jnp.float32)
            for ref in [e0, e1] + [jx.at[w] for w in range(views)]:
                clear(ref, halo, 0, wide)

    for edge, lo, hi in ((me == 0, 0, HALO), (me == strips - 1, HALO + strip, wide)):
        @pl.when(edge)
        def _(lo=lo, hi=hi):
            clear(e1, (0, 3 * CZ), lo, hi)
            for w in range(views):
                clear(jx.at[w], (CZ, 2 * CZ), lo, hi)

    pl.semaphore_wait(barrier, amount)

    def span(c):
        start = 0 if c == 0 else CZ + c * CP * rows
        return pl.ds(start, CZ + (c + 1) * CP * rows - start)

    def up_copy(src, t, c):
        return pltpu.make_async_remote_copy(
            src_ref=src.at[t, span(c)], dst_ref=ru.at[t, span(c)], send_sem=us.at[t, c],
            recv_sem=ur.at[t, c], device_id={"gz": z + 1}, device_id_type=MESH)

    def down_copy(src, t, c):
        return pltpu.make_async_remote_copy(
            src_ref=src.at[t, span(c)], dst_ref=rd.at[t, span(c)], send_sem=ds_.at[t, c],
            recv_sem=dr.at[t, c], device_id={"gz": z - 1}, device_id_type=MESH)

    @pl.when(z == 0)
    def _():
        @pl.loop(0, slabs - 1)
        def _(k):
            for c in range(NCH):
                up_copy(acc_ref, slabs - 1 - k, c).start()

    @pl.when(z == slabs - 1)
    def _():
        @pl.loop(0, slabs - 1)
        def _(k):
            for c in range(NCH):
                down_copy(acc_ref, k, c).start()

    own_tap = pltpu.make_async_copy(tap_in, tap_all.at[v], loc_sem)
    own_tap.start()

    def tap_copy(d):
        return pltpu.make_async_remote_copy(
            src_ref=tap_in, dst_ref=tap_all.at[v], send_sem=tap_s.at[d - 1],
            recv_sem=tap_r.at[d - 1], device_id={"view": (v + d) % views}, device_id_type=MESH)

    for d in range(1, views):
        tap_copy(d).start()

    @pl.loop(0, slabs - 1)
    def _(k):
        t_up, t_down = slabs - 1 - k, k
        for c in range(NCH):
            at = span(c)

            @pl.when(below & (t_up > z))
            def _():
                up_copy(ru, t_up, c).wait_recv()
                ru[t_up, at] = ru[t_up, at] + acc_ref[t_up, at]
                up_copy(ru, t_up, c).start()

            @pl.when(above & (t_down < z))
            def _():
                down_copy(rd, t_down, c).wait_recv()
                rd[t_down, at] = rd[t_down, at] + acc_ref[t_down, at]
                down_copy(rd, t_down, c).start()

    own_tap.wait()
    for d in range(1, views):
        tap_copy(d).wait()

    apart = lax.broadcasted_iota(jnp.int32, (128, 128), 0) - lax.broadcasted_iota(jnp.int32, (128, 128), 1)

    @pl.loop(0, views)
    def _(w):
        ahead = jnp.zeros((128, 128), jnp.float32)
        back = jnp.zeros((128, 128), jnp.float32)
        for t in range(taps):
            tap = tap_all[w, 2 * taps + t : 2 * taps + t + 1, :]
            ahead = jnp.where(apart == t - margin, tap, ahead)
            back = jnp.where(apart == margin - t, tap, back)
        for n, full in enumerate((ahead, back)):
            top = full.astype(jnp.bfloat16)
            kx[w, n, 0:128, 0:128] = top
            kx[w, n, 128:256, 0:128] = top
            kx[w, n, 0:128, 128:256] = (full - top.astype(jnp.float32)).astype(jnp.bfloat16)
            kx[w, n, 128:256, 128:256] = jnp.zeros((128, 128), jnp.bfloat16)

    fy, fx = [tap_in[3 * taps + n : 3 * taps + n + 1, :] for n in (1, 2)]
    last_row = lax.broadcasted_iota(jnp.int32, (rows, 128), 0) == rows - 1
    last_col = lax.broadcasted_iota(jnp.int32, (rows, 128), 1) == 127
    joined = joined_ref.at[0]
    mid = pl.ds(CZ, CZ)

    def planes_of(c):
        return pl.ds(c * CP, CP), pl.ds(CZ + c * CP, CP)

    def piece(i):
        lo, hi = max(i * strip - HALO, 0), min((i + 1) * strip + HALO, rows)
        return (lo, hi), (lo - i * strip + HALO, hi - i * strip + HALO)

    low_edge = ((rows - HALO, rows), (0, HALO))
    high_edge = ((0, HALO), (HALO + strip, wide))

    def part_copy(c, w, rows_of, target, send, recv):
        src_p, dst_p = planes_of(c)
        (lo, hi), (dlo, dhi) = rows_of
        return pltpu.make_async_remote_copy(
            src_ref=joined.at[src_p, pl.ds(lo, hi - lo), :], dst_ref=jx.at[w, dst_p, pl.ds(dlo, dhi - dlo), :],
            send_sem=send, recv_sem=recv, device_id=strip_dev(z, target), device_id_type=MESH)

    def sends(c):
        out = []
        for i in range(views):
            out.append((g * views + i, z >= 0, piece(i), ms.at[i, c], mr.at[v, c]))
        out.append(((g + 1) * views, g < bands - 1, low_edge, los.at[c], lor.at[v, c]))
        out.append((g * views - 1, g > 0, high_edge, his.at[c], hir.at[v, c]))
        return out

    def join(c):
        src_p, _ = planes_of(c)

        @pl.when(below)
        def _():
            up_copy(acc_ref, z, c).wait_recv()

        @pl.when(above)
        def _():
            down_copy(acc_ref, z, c).wait_recv()

        for p in range(c * CP, (c + 1) * CP):
            at = pl.ds(CZ + p * rows, rows)
            total = acc_ref[z, at, :] + ru[z, at, :] + rd[z, at, :]
            cnt = pl.ds(p, 1)
            covered = acc_ref[z, cnt, :] + ru[z, cnt, :] + rd[z, cnt, :]
            follow = jnp.where(last_row, total, pltpu.roll(total, rows - 1, 0))
            total = (1.0 - fy) * total + fy * follow
            follow = jnp.where(last_col, total, pltpu.roll(total, 127, 1))
            total = (1.0 - fx) * total + fx * follow
            joined_ref[0, p] = jnp.maximum(total / (covered + 1.0), DATA_FLOOR)
        for target, ok, rows_of, send, recv in sends(c):
            (lo, hi), (dlo, dhi) = rows_of

            @pl.when(ok & (target != me))
            def _(rows_of=rows_of, target=target, send=send, recv=recv):
                part_copy(c, v, rows_of, target, send, recv).start()

            @pl.when(ok & (target == me))
            def _(lo=lo, hi=hi, dlo=dlo, dhi=dhi):
                for p in range(c * CP, (c + 1) * CP):
                    jx[v, CZ + p, dlo:dhi, :] = joined_ref[0, p, lo:hi, :]

    def z_copy(ref, w, c, up, send, recv):
        dst = (0 if up else 2 * CZ) + c * CP
        src = CZ + c * CP
        a, b = ref.at[pl.ds(src, CP)], ref.at[pl.ds(dst, CP)]
        return pltpu.make_async_remote_copy(
            src_ref=a, dst_ref=b, send_sem=send, recv_sem=recv,
            device_id={"gz": z + 1 if up else z - 1}, device_id_type=MESH)

    def z_copies(c, up):
        side = 1 if up else 0
        near = c * CP >= CZ - margin if up else c * CP < margin
        if near:
            return [z_copy(jx.at[w], w, c, up, zs.at[side, w, c], zr.at[side, w, c]) for w in range(views)]
        return [z_copy(e0, 0, c, up, zs.at[side, 0, c], zr.at[side, 0, c])]

    def average(p):
        total = jx[0, p]
        for w in range(1, views):
            total = total + jx[w, p]
        e0[p] = total / views

    def spread(c):
        for w in range(views):
            for i in range(views):
                @pl.when((idx == i) & ((w != v) | (band != g)))
                def _(i=i, w=w):
                    part_copy(c, w, piece(i), me, ms.at[i, c], mr.at[w, c]).wait_recv()

            @pl.when((idx == 0) & (band > 0) & ((w != v) | (band - 1 != g)))
            def _(w=w):
                part_copy(c, w, low_edge, me, los.at[c], lor.at[w, c]).wait_recv()

            @pl.when((idx == views - 1) & (band < bands - 1) & ((w != v) | (band + 1 != g)))
            def _(w=w):
                part_copy(c, w, high_edge, me, his.at[c], hir.at[w, c]).wait_recv()

        for p in range(c * CP, (c + 1) * CP):
            average(CZ + p)
        for up, ok in ((True, above), (False, below)):
            @pl.when(ok)
            def _(up=up):
                for copy in z_copies(c, up):
                    copy.start()

    join(0)
    for c in range(1, NCH):
        join(c)
        spread(c - 1)
    spread(NCH - 1)

    for c in range(NCH):
        for up, ok in ((True, below), (False, above)):
            @pl.when(ok)
            def _(up=up, c=c):
                copies = z_copies(c, up)
                for copy in copies:
                    copy.wait_recv()
                if len(copies) == views and views > 1:
                    for p in range(c * CP, (c + 1) * CP):
                        average((0 if up else 2 * CZ) + p)

    planes_r = CZ + 2 * margin
    rows_r = strip + 2 * margin

    def along_x(u, w, n):
        top = u.astype(jnp.bfloat16)
        rest = (u - top.astype(jnp.float32)).astype(jnp.bfloat16)
        both = jnp.dot(jnp.concatenate([top, rest], axis=1), kx[w, n], preferred_element_type=jnp.float32)
        return both[:, 0:128] + both[:, 128:256]

    def weighted(terms, weights):
        total = weights[0] * terms[0]
        for term, weight in zip(terms[1:], weights[1:]):
            total = total + weight * term
        return total

    def correct(est, emit):
        for w in range(views):
            def tap(axis, t):
                at = axis * taps + t
                return tap_all[w, at : at + 1, :]

            @pl.loop(0, wide // 8, unroll=2)
            def _(r):
                at = pl.ds(pl.multiple_of(r * 8, 8), 8)
                column = [est[CZ - 2 * margin + p, at, :] for p in range(planes_r + 2 * margin)]
                for p in range(planes_r):
                    za[p, at, :] = weighted(column[p : p + taps], [tap(0, t) for t in range(taps)])

            @pl.loop(0, planes_r, unroll=4)
            def _(p):
                base = HALO - 2 * margin
                zb[p] = weighted([za[p, base + t : base + t + rows_r, :] for t in range(taps)],
                                 [tap(1, t) for t in range(taps)])

            @pl.loop(0, planes_r // 4)
            def _(c):
                at = pl.ds(c * 4, 4)
                blurred = along_x(zb[at].reshape(4 * rows_r, 128), w, 0).reshape(4, rows_r, 128)
                data = jx[w, pl.ds(c * 4 + CZ - margin, 4), HALO - margin : HALO - margin + rows_r, :]
                rt[at] = jnp.where(data > 0.0, data / blurred, 0.0)

            @pl.loop(0, rows_r // 8, unroll=True)
            def _(r):
                at = pl.ds(pl.multiple_of(r * 8, 8), 8)
                column = [rt[p, at, :] for p in range(planes_r)]
                for p in range(CZ):
                    za[p, at, :] = weighted(column[p : p + taps], [tap(0, taps - 1 - t) for t in range(taps)])

            @pl.loop(0, CZ, unroll=4)
            def _(p):
                yb[p] = weighted([za[p, t : t + strip, :] for t in range(taps)],
                                 [tap(1, taps - 1 - t) for t in range(taps)])

            for c in range(NOUT):
                at = pl.ds(c * OC, OC)
                logs = jnp.log(along_x(yb[at].reshape(OC * strip, 128), w, 1)).reshape(OC, strip, 128)
                if w > 0:
                    logs = lg[at] + logs
                if w < views - 1:
                    lg[at] = logs
                else:
                    emit(c, est[pl.ds(CZ + c * OC, OC), HALO : HALO + strip, :] * jnp.exp(logs / views))

    inner = pl.ds(HALO, strip)
    near = []
    for n, (dz, ds) in enumerate([(a, b) for a in (-1, 1, 0) for b in (0, -1, 1) if a or b]):
        zok = {-1: below, 0: z >= 0, 1: above}[dz]
        sok = {-1: left, 0: z >= 0, 1: right}[ds]
        far_z = {-1: above, 0: z >= 0, 1: below}[dz]
        far_s = {-1: right, 0: z >= 0, 1: left}[ds]
        near.append((n, dz, ds, zok & sok, far_z & far_s))

    def near_copy(n, dz, ds, c):
        src_r = {-1: pl.ds(HALO, HALO), 0: inner, 1: pl.ds(strip, HALO)}[ds]
        dst_r = {-1: pl.ds(HALO + strip, HALO), 0: inner, 1: pl.ds(0, HALO)}[ds]
        dst = {-1: 2 * CZ, 0: CZ, 1: 0}[dz] + c * OC
        return pltpu.make_async_remote_copy(
            src_ref=e1.at[pl.ds(CZ + c * OC, OC), src_r, :], dst_ref=e1.at[pl.ds(dst, OC), dst_r, :],
            send_sem=es.at[n, c], recv_sem=er.at[n, c], device_id=strip_dev(z + dz, me + ds), device_id_type=MESH)

    def emit_step(c, new):
        e1[pl.ds(CZ + c * OC, OC), HALO : HALO + strip, :] = new
        for n, dz, ds, ok, _ in near:
            @pl.when(ok)
            def _(n=n, dz=dz, ds=ds):
                near_copy(n, dz, ds, c).start()

    correct(e0, emit_step)
    for c in range(NOUT):
        for n, dz, ds, _, ok in near:
            @pl.when(ok)
            def _(n=n, dz=dz, ds=ds, c=c):
                near_copy(n, dz, ds, c).wait_recv()

    def out_copy(c, w, target_g, i):
        at = pl.ds(pl.multiple_of(i * strip, 8), strip)
        part = pl.ds(c * OC, OC)
        return pltpu.make_async_remote_copy(
            src_ref=lg.at[part], dst_ref=est_ref.at[part, at, :], send_sem=out_s.at[w, c],
            recv_sem=out_r.at[i, c], device_id=dev(z, w, target_g), device_id_type=MESH)

    def emit_last(c, new):
        lg[pl.ds(c * OC, OC)] = new
        for w in range(views):
            away = (w != v) | (band != g)

            @pl.when(away)
            def _(w=w):
                out_copy(c, w, band, idx).start()

            @pl.when(jnp.logical_not(away))
            def _():
                est_ref[pl.ds(c * OC, OC), pl.ds(pl.multiple_of(idx * strip, 8), strip), :] = new

    correct(e1, emit_last)
    for c in range(NOUT):
        for i in range(views):
            @pl.when(g * views + i != me)
            def _(i=i, c=c):
                out_copy(c, 0, g, i).wait_recv()

    for c in range(NOUT):
        for w in range(views):
            @pl.when((w != v) | (band != g))
            def _(w=w, c=c):
                out_copy(c, w, band, idx).wait_send()

    @pl.loop(0, slabs)
    def _(t):
        for c in range(NCH):
            @pl.when(t > z)
            def _():
                up_copy(acc_ref, t, c).wait_send()

            @pl.when(t < z)
            def _():
                down_copy(acc_ref, t, c).wait_send()

    for c in range(NCH):
        for target, ok, rows_of, send, recv in sends(c):
            @pl.when(ok & (target != me))
            def _(rows_of=rows_of, target=target, send=send, recv=recv, c=c):
                part_copy(c, v, rows_of, target, send, recv).wait_send()

        for up, ok in ((True, above), (False, below)):
            @pl.when(ok)
            def _(up=up, c=c):
                for copy in z_copies(c, up):
                    copy.wait_send()

    for c in range(NOUT):
        for n, dz, ds, ok, _ in near:
            @pl.when(ok)
            def _(n=n, dz=dz, ds=ds, c=c):
                near_copy(n, dz, ds, c).wait_send()


def on_device(dims, camera, background, destination, offsets, shift_frac, psf_taps):
    slabs, views, bands = dims
    blocks, planes, rows, cols = camera.shape[1:]
    taps = psf_taps.shape[-1]
    margin = taps // 2
    tall = CZ * rows + CZ
    strip = rows // views
    wide = strip + 2 * HALO
    tap_rows = -(-3 * (taps + 1) // 8) * 8
    vmem = pl.BlockSpec(memory_space=pltpu.VMEM)
    hbm = functools.partial(pltpu.with_memory_space_constraint, memory_space=pltpu.HBM)
    cell = 4 * cols
    room = 2 * 1024 * 1024
    acc, tap_rows_all = pl.pallas_call(
        functools.partial(deposit_kernel, rows),
        in_specs=[pl.BlockSpec(memory_space=pltpu.HBM)] * 6,
        out_specs=(vmem, vmem),
        out_shape=(
            pltpu.VMEM((slabs, tall, cols), jnp.float32),
            pltpu.VMEM((tap_rows, cols), jnp.float32),
        ),
        scratch_shapes=[
            pltpu.SMEM((blocks,), jnp.int32),
            pltpu.SMEM((blocks,), jnp.int32),
            pltpu.SMEM((1, 1, 1), jnp.int32),
            pltpu.SMEM((3,), jnp.float32),
            pltpu.VMEM((3, 1, taps), jnp.float32),
            pltpu.VMEM((blocks, planes, rows, cols), jnp.float32),
            pltpu.SemaphoreType.DMA((blocks // CHUNK,)),
            pltpu.SemaphoreType.DMA((5,)),
        ],
        compiler_params=pltpu.CompilerParams(
            vmem_limit_bytes=cell * (blocks * planes * rows + slabs * tall) + room),
        name="deposit",
    )(hbm(destination.reshape(-1)), hbm(offsets.reshape(-1)), background, hbm(shift_frac[0]),
      hbm(jnp.transpose(psf_taps, (1, 0, 2))), hbm(camera[0]))

    dma = pltpu.SemaphoreType.DMA
    f32 = jnp.float32
    shapes = [
        (slabs, tall, cols), (slabs, tall, cols), (views, tap_rows, cols),
        (views, 3 * CZ, wide, cols), (3 * CZ, wide, cols), (3 * CZ, wide, cols),
    ]
    late = [
        (CZ + 2 * margin, wide, cols),
        (CZ + 2 * margin, strip + 2 * margin, cols), (CZ + 2 * margin, strip + 2 * margin, cols),
        (CZ, strip, cols), (CZ, strip, cols),
    ]
    total = sum([functools.reduce(lambda a, b: a * b, s) for s in shapes + late])
    total = total + cols * (slabs * tall + 2 * CZ * rows + views * 4 * cols)
    estimate, joined = pl.pallas_call(
        functools.partial(world_kernel, dims, rows, taps),
        in_specs=[vmem, vmem],
        out_specs=(vmem, vmem),
        out_shape=(
            jax.ShapeDtypeStruct((CZ, rows, cols), f32),
            jax.ShapeDtypeStruct((1, CZ, rows, cols), f32),
        ),
        scratch_shapes=[pltpu.VMEM(s, f32) for s in shapes]
        + [pltpu.VMEM((views, 2, 2 * cols, 2 * cols), jnp.bfloat16)]
        + [pltpu.VMEM(s, f32) for s in late]
        + [
            dma((slabs, NCH)), dma((slabs, NCH)), dma((slabs, NCH)), dma((slabs, NCH)),
            dma((views,)), dma((views,)), dma,
            dma((views, NCH)), dma((views, NCH)), dma((NCH,)), dma((views, NCH)), dma((NCH,)), dma((views, NCH)),
            dma((2, views, NCH)), dma((2, views, NCH)), dma((8, NOUT)), dma((8, NOUT)),
            dma((views, NOUT)), dma((views, NOUT)),
        ],
        compiler_params=pltpu.CompilerParams(
            collective_id=0, has_side_effects=True, vmem_limit_bytes=4 * total + room),
        name="world",
    )(acc, tap_rows_all)
    return estimate, joined


def solution(mesh):
    dims = (mesh.shape["gz"], mesh.shape["view"], mesh.shape["gy"])
    return jax.shard_map(
        functools.partial(on_device, dims),
        mesh=mesh,
        in_specs=(
            P("view", ("groups", "gz"), None, "gy", None),
            P("view", "gy", ("groups", "gz")),
            P("view", "gy", ("groups", "gz"), None),
            P("view", "gy", ("groups", "gz")),
            P("view", None),
            P("view", None, None),
        ),
        out_specs=(P(("groups", "gz"), "gy", None), P("view", ("groups", "gz"), "gy", None)),
        check_vma=False,
    )
```

time: 67.8 us -> 72.1 us (1.063)
  the two profiles are of different devices: /device:TPU:8 before, /device:TPU:1 now
where the time goes in v1:
time: 72.1 us; the launch traced here: 72 us
  Pallas kernels  69.3 us (96%)
  local copies, waits for them, and re-layouts  1.41 us (2%)
  between operations  1.29 us (2%)
    pallas_call x1, Pallas kernels, on_device(): pl.pallas_call(functools.partial(world_kernel, dims, rows, taps), in_spec...  66.8 us
    pallas_call x1, Pallas kernels, on_device(): pl.pallas_call(functools.partial(deposit_kernel, rows), in_specs=[pl.Bloc...  2.44 us

profile of v1, /device:TPU:1, one launch (start us, length us, event | category | flops | bytes accessed | tf_op | source)
XLA Modules:
  0.0 72.0 jit_solution(5914641465775375719)
XLA Ops:
  1.3 2.4 %deposit.1 = (f32[4,520,128]{2,1,0:T(8,128)S(1)}, f32[32,128]{1,0:T(8,128)S(1)}) custom-call(s32[32]{0:T(128)} %bitcast.7, s32[32]{0:T(128)} %bitcast.8, s32[1,1,1]{2,1,0:T(1,128)S(6)} %copy.10.level_in, f32[3]{0:T(128)} %bitcast.9, f32[3,1,9]{2,1,0:T(1,128)} %bitcast.6, f32[32,3,64,128]{3,2,1,0:T(8,128)} %bitcast.5), custom_call_target="tpu_custom_call" | custom-call | tf_op jit(solution)/shard_map/deposit/pallas_call | solution.py:517
  3.7 66.8 %world.1 = (f32[8,64,128]{2,1,0:T(8,128)S(1)}, f32[1,8,64,128]{3,2,1,0:T(8,128)S(1)}) custom-call(f32[4,520,128]{2,1,0:T(8,128)S(1)} %get-tuple-element.4.acc_ref, f32[32,128]{1,0:T(8,128)S(1)} %get-tuple-element.5.tap_in), custom_call_target="tpu_custom_call" | custom-call | tf_op jit(solution)/shard_map/world/pallas_call | solution.py:554
  70.6 0.7 copy.11
  71.3 0.7 copy.12

commit v2 on v1

--- a/solution.py
+++ b/solution.py
@@ -180,23 +180,35 @@
     for d in range(1, views):
         tap_copy(d).start()
 
+    def pass_on(copy, ref, t, ok):
+        @pl.when(ok)
+        def _():
+            for c in range(NCH):
+                at = span(c)
+                copy(ref, t, c).wait_recv()
+                ref[t, at] = ref[t, at] + acc_ref[t, at]
+                copy(ref, t, c).start()
+
+    def pass_up(k):
+        t = slabs - 1 - k
+        pass_on(up_copy, ru, t, below & (t > z))
+
+    def pass_down(k):
+        pass_on(down_copy, rd, k, above & (k < z))
+
     @pl.loop(0, slabs - 1)
     def _(k):
-        t_up, t_down = slabs - 1 - k, k
-        for c in range(NCH):
-            at = span(c)
-
-            @pl.when(below & (t_up > z))
-            def _():
-                up_copy(ru, t_up, c).wait_recv()
-                ru[t_up, at] = ru[t_up, at] + acc_ref[t_up, at]
-                up_copy(ru, t_up, c).start()
-
-            @pl.when(above & (t_down < z))
-            def _():
-                down_copy(rd, t_down, c).wait_recv()
-                rd[t_down, at] = rd[t_down, at] + acc_ref[t_down, at]
-                down_copy(rd, t_down, c).start()
+        low = 2 * z < slabs
+
+        @pl.when(low)
+        def _():
+            pass_up(k)
+            pass_down(k)
+
+        @pl.when(jnp.logical_not(low))
+        def _():
+            pass_down(k)
+            pass_up(k)
 
     own_tap.wait()
     for d in range(1, views):

time: 72.1 us -> 54.1 us (0.75)
  Pallas kernels: 69.3 us -> 51.3 us
    pallas_call x1, Pallas kernels: 66.8 us -> 48.8 us  [on_device(): pl.pallas_call(functools.partial(world_kernel, dims, rows, taps), in_spec...]
where the time goes in v2:
time: 54.1 us; the launch traced here: 54 us
  Pallas kernels  51.3 us (95%)
  local copies, waits for them, and re-layouts  1.41 us (3%)
  between operations  1.29 us (2%)
    pallas_call x1, Pallas kernels, on_device(): pl.pallas_call(functools.partial(world_kernel, dims, rows, taps), in_spec...  48.8 us
    pallas_call x1, Pallas kernels, on_device(): pl.pallas_call(functools.partial(deposit_kernel, rows), in_specs=[pl.Bloc...  2.44 us
    unnamed x2, local copies, waits for them, and re-layouts  1.41 us

profile of v2, /device:TPU:1, one launch (start us, length us, event | category | flops | bytes accessed | tf_op | source)
XLA Modules:
  0.0 54.0 jit_solution(15903972754777583433)
XLA Ops:
  1.3 2.4 %deposit.1 = (f32[4,520,128]{2,1,0:T(8,128)S(1)}, f32[32,128]{1,0:T(8,128)S(1)}) custom-call(s32[32]{0:T(128)} %bitcast.7, s32[32]{0:T(128)} %bitcast.8, s32[1,1,1]{2,1,0:T(1,128)S(6)} %copy.10.level_in, f32[3]{0:T(128)} %bitcast.9, f32[3,1,9]{2,1,0:T(1,128)} %bitcast.6, f32[32,3,64,128]{3,2,1,0:T(8,128)} %bitcast.5), custom_call_target="tpu_custom_call" | custom-call | tf_op jit(solution)/shard_map/deposit/pallas_call | solution.py:529
  3.7 48.8 %world.1 = (f32[8,64,128]{2,1,0:T(8,128)S(1)}, f32[1,8,64,128]{3,2,1,0:T(8,128)S(1)}) custom-call(f32[4,520,128]{2,1,0:T(8,128)S(1)} %get-tuple-element.4.acc_ref, f32[32,128]{1,0:T(8,128)S(1)} %get-tuple-element.5.tap_in), custom_call_target="tpu_custom_call" | custom-call | tf_op jit(solution)/shard_map/world/pallas_call | solution.py:566
  52.6 0.7 %copy.11 = f32[8,64,128]{2,1,0:T(8,128)} copy(f32[8,64,128]{2,1,0:T(8,128)S(1)} %get-tuple-element.8) | data formatting | bytes 524288
  53.3 0.7 %copy.12 = f32[1,8,64,128]{3,2,1,0:T(8,128)} copy(f32[1,8,64,128]{3,2,1,0:T(8,128)S(1)} %get-tuple-element.9) | data formatting | bytes 524288

commit v3 on v2

--- a/solution.py
+++ b/solution.py
@@ -17,6 +17,7 @@
 NOUT = CZ // OC
 
 DATA_FLOOR = 0.25
+TINY = 1e-30
 MESH = pl.DeviceIdType.MESH
 
 
@@ -78,7 +79,7 @@
 def world_kernel(
     dims, rows, taps,
     acc_ref, tap_in, est_ref, joined_ref,
-    ru, rd, tap_all, jx, e0, e1, kx, za, zb, rt, yb, lg,
+    ru, rd, tap_all, jx, e0, e1, kx, za, zb, rt, yb, part, lg,
     us, ur, ds_, dr, tap_s, tap_r, loc_sem, ms, mr, los, lor, his, hir,
     zs, zr, es, er, out_s, out_r,
 ):
@@ -371,9 +372,19 @@
             total = total + weight * term
         return total
 
+    def root(terms):
+        if len(terms) == 1:
+            return terms[0]
+        if len(terms) % 2:
+            total = jnp.log(terms[0])
+            for term in terms[1:]:
+                total = total + jnp.log(term)
+            return jnp.exp(total / len(terms))
+        return root([jnp.sqrt(a * b) for a, b in zip(terms[0::2], terms[1::2])])
+
     def correct(est, emit):
         for w in range(views):
-            def tap(axis, t):
+            def tap(axis, t, w=w):
                 at = axis * taps + t
                 return tap_all[w, at : at + 1, :]
 
@@ -395,29 +406,26 @@
                 at = pl.ds(c * 4, 4)
                 blurred = along_x(zb[at].reshape(4 * rows_r, 128), w, 0).reshape(4, rows_r, 128)
                 data = jx[w, pl.ds(c * 4 + CZ - margin, 4), HALO - margin : HALO - margin + rows_r, :]
-                rt[at] = jnp.where(data > 0.0, data / blurred, 0.0)
-
-            @pl.loop(0, rows_r // 8, unroll=True)
-            def _(r):
-                at = pl.ds(pl.multiple_of(r * 8, 8), 8)
-                column = [rt[p, at, :] for p in range(planes_r)]
-                for p in range(CZ):
-                    za[p, at, :] = weighted(column[p : p + taps], [tap(0, taps - 1 - t) for t in range(taps)])
-
-            @pl.loop(0, CZ, unroll=4)
-            def _(p):
-                yb[p] = weighted([za[p, t : t + strip, :] for t in range(taps)],
-                                 [tap(1, taps - 1 - t) for t in range(taps)])
-
-            for c in range(NOUT):
-                at = pl.ds(c * OC, OC)
-                logs = jnp.log(along_x(yb[at].reshape(OC * strip, 128), w, 1)).reshape(OC, strip, 128)
-                if w > 0:
-                    logs = lg[at] + logs
-                if w < views - 1:
-                    lg[at] = logs
-                else:
-                    emit(c, est[pl.ds(CZ + c * OC, OC), HALO : HALO + strip, :] * jnp.exp(logs / views))
+                blurred = jnp.maximum(blurred, TINY)
+                inverse = pl.reciprocal(blurred, approx=True)
+                inverse = inverse * (2.0 - blurred * inverse)
+                rt[w, at] = data * inverse
+
+        for c in range(NOUT):
+            for w in range(views):
+                def tap(axis, t, w=w):
+                    at = axis * taps + taps - 1 - t
+                    return tap_all[w, at : at + 1, :]
+
+                for r in range(rows_r // 8):
+                    at = pl.ds(r * 8, 8)
+                    column = [rt[w, c * OC + p, at, :] for p in range(OC + 2 * margin)]
+                    for p in range(OC):
+                        za[p, at, :] = weighted(column[p : p + taps], [tap(0, t) for t in range(taps)])
+                for p in range(OC):
+                    yb[p] = weighted([za[p, t : t + strip, :] for t in range(taps)], [tap(1, t) for t in range(taps)])
+                part[w] = along_x(yb[...].reshape(OC * strip, 128), w, 1).reshape(OC, strip, 128)
+            emit(c, est[pl.ds(CZ + c * OC, OC), HALO : HALO + strip, :] * root([part[w] for w in range(views)]))
 
     inner = pl.ds(HALO, strip)
     near = []
@@ -444,6 +452,30 @@
                 near_copy(n, dz, ds, c).start()
 
     correct(e0, emit_step)
+
+    @pl.loop(0, slabs)
+    def _(t):
+        for c in range(NCH):
+            @pl.when(t > z)
+            def _():
+                up_copy(acc_ref, t, c).wait_send()
+
+            @pl.when(t < z)
+            def _():
+                down_copy(acc_ref, t, c).wait_send()
+
+    for c in range(NCH):
+        for target, ok, rows_of, send, recv in sends(c):
+            @pl.when(ok & (target != me))
+            def _(rows_of=rows_of, target=target, send=send, recv=recv, c=c):
+                part_copy(c, v, rows_of, target, send, recv).wait_send()
+
+        for up, ok in ((True, above), (False, below)):
+            @pl.when(ok)
+            def _(up=up, c=c):
+                for copy in z_copies(c, up):
+                    copy.wait_send()
+
     for c in range(NOUT):
         for n, dz, ds, _, ok in near:
             @pl.when(ok)
@@ -471,6 +503,13 @@
                 est_ref[pl.ds(c * OC, OC), pl.ds(pl.multiple_of(idx * strip, 8), strip), :] = new
 
     correct(e1, emit_last)
+
+    for c in range(NOUT):
+        for n, dz, ds, ok, _ in near:
+            @pl.when(ok)
+            def _(n=n, dz=dz, ds=ds, c=c):
+                near_copy(n, dz, ds, c).wait_send()
+
     for c in range(NOUT):
         for i in range(views):
             @pl.when(g * views + i != me)
@@ -482,35 +521,6 @@
             @pl.when((w != v) | (band != g))
             def _(w=w, c=c):
                 out_copy(c, w, band, idx).wait_send()
-
-    @pl.loop(0, slabs)
-    def _(t):
-        for c in range(NCH):
-            @pl.when(t > z)
-            def _():
-                up_copy(acc_ref, t, c).wait_send()
-
-            @pl.when(t < z)
-            def _():
-                down_copy(acc_ref, t, c).wait_send()
-
-    for c in range(NCH):
-        for target, ok, rows_of, send, recv in sends(c):
-            @pl.when(ok & (target != me))
-            def _(rows_of=rows_of, target=target, send=send, recv=recv, c=c):
-                part_copy(c, v, rows_of, target, send, recv).wait_send()
-
-        for up, ok in ((True, above), (False, below)):
-            @pl.when(ok)
-            def _(up=up, c=c):
-                for copy in z_copies(c, up):
-                    copy.wait_send()
-
-    for c in range(NOUT):
-        for n, dz, ds, ok, _ in near:
-            @pl.when(ok)
-            def _(n=n, dz=dz, ds=ds, c=c):
-                near_copy(n, dz, ds, c).wait_send()
 
 
 def on_device(dims, camera, background, destination, offsets, shift_frac, psf_taps):
@@ -558,8 +568,8 @@
     ]
     late = [
         (CZ + 2 * margin, wide, cols),
-        (CZ + 2 * margin, strip + 2 * margin, cols), (CZ + 2 * margin, strip + 2 * margin, cols),
-        (CZ, strip, cols), (CZ, strip, cols),
+        (CZ + 2 * margin, strip + 2 * margin, cols), (views, CZ + 2 * margin, strip + 2 * margin, cols),
+        (OC, strip, cols), (views, OC, strip, cols), (CZ, strip, cols),
     ]
     total = sum([functools.reduce(lambda a, b: a * b, s) for s in shapes + late])
     total = total + cols * (slabs * tall + 2 * CZ * rows + views * 4 * cols)

time: 54.1 us -> 53.3 us (0.985)
  Pallas kernels: 51.3 us -> 50.4 us
    pallas_call x1, Pallas kernels: 48.8 us -> 48 us  [on_device(): pl.pallas_call(functools.partial(world_kernel, dims, rows, taps), in_spec...]
where the time goes in v3:
time: 53.3 us; the launch traced here: 53.1 us
  Pallas kernels  50.4 us (95%)
  local copies, waits for them, and re-layouts  1.41 us (3%)
  between operations  1.29 us (2%)
    pallas_call x1, Pallas kernels, on_device(): pl.pallas_call(functools.partial(world_kernel, dims, rows, taps), in_spec...  48 us
    pallas_call x1, Pallas kernels, on_device(): pl.pallas_call(functools.partial(deposit_kernel, rows), in_specs=[pl.Bloc...  2.44 us
    unnamed x2, local copies, waits for them, and re-layouts  1.41 us

profile of v3, /device:TPU:1, one launch (start us, length us, event | category | flops | bytes accessed | tf_op | source)
XLA Modules:
  0.0 53.1 jit_solution(13121524970018219292)
XLA Ops:
  1.3 2.4 %deposit.1 = (f32[4,520,128]{2,1,0:T(8,128)S(1)}, f32[32,128]{1,0:T(8,128)S(1)}) custom-call(s32[32]{0:T(128)} %bitcast.7, s32[32]{0:T(128)} %bitcast.8, s32[1,1,1]{2,1,0:T(1,128)S(6)} %copy.10.level_in, f32[3]{0:T(128)} %bitcast.9, f32[3,1,9]{2,1,0:T(1,128)} %bitcast.6, f32[32,3,64,128]{3,2,1,0:T(8,128)} %bitcast.5), custom_call_target="tpu_custom_call" | custom-call | tf_op jit(solution)/shard_map/deposit/pallas_call | solution.py:539
  3.7 48.0 %world.1 = (f32[8,64,128]{2,1,0:T(8,128)S(1)}, f32[1,8,64,128]{3,2,1,0:T(8,128)S(1)}) custom-call(f32[4,520,128]{2,1,0:T(8,128)S(1)} %get-tuple-element.4.acc_ref, f32[32,128]{1,0:T(8,128)S(1)} %get-tuple-element.5.tap_in), custom_call_target="tpu_custom_call" | custom-call | tf_op jit(solution)/shard_map/world/pallas_call | solution.py:576
  51.7 0.7 %copy.11 = f32[8,64,128]{2,1,0:T(8,128)} copy(f32[8,64,128]{2,1,0:T(8,128)S(1)} %get-tuple-element.8) | data formatting | bytes 524288
  52.4 0.7 %copy.12 = f32[1,8,64,128]{3,2,1,0:T(8,128)} copy(f32[1,8,64,128]{3,2,1,0:T(8,128)S(1)} %get-tuple-element.9) | data formatting | bytes 524288

commit v4 on v3

--- a/solution.py
+++ b/solution.py
@@ -10,7 +10,7 @@
 CZ = 8
 ITERS = 2
 HALO = 8
-CHUNK = 4
+BAND = 8
 CP = 2
 NCH = CZ // CP
 OC = 4
@@ -21,68 +21,25 @@
 MESH = pl.DeviceIdType.MESH
 
 
-def deposit_kernel(
-    rows, dest_in, offs_in, level_in, frac_in, psf_in, cam_ref, acc_ref, tap_ref,
-    dest, offs, level, frac, psf, cam, sems, small,
-):
-    taps = psf.shape[2]
-    blocks, planes = cam_ref.shape[:2]
-    pairs = ((dest_in, dest), (offs_in, offs), (level_in, level), (frac_in, frac), (psf_in, psf))
-    copies = [pltpu.make_async_copy(a, b, small.at[n]) for n, (a, b) in enumerate(pairs)]
-    for copy in copies:
-        copy.start()
-
-    def fetch(c):
-        at = pl.ds(c * CHUNK, CHUNK)
-        return pltpu.make_async_copy(cam_ref.at[at], cam.at[at], sems.at[c])
-
-    for c in range(blocks // CHUNK):
-        fetch(c).start()
-
-    @pl.loop(0, acc_ref.shape[0])
-    def _(s):
-        acc_ref[s] = jnp.zeros(acc_ref.shape[1:], jnp.float32)
-
-    for copy in copies:
-        copy.wait()
-
-    tap_ref[...] = jnp.zeros(tap_ref.shape, jnp.float32)
-    for axis in range(3):
-        scale = jnp.sum(psf[axis], axis=1, keepdims=True)
-        share = psf[axis] / scale
-        for t in range(taps):
-            at = axis * taps + t
-            tap_ref[at : at + 1, :] = jnp.broadcast_to(share[:, t : t + 1], (1, 128))
-        at = 3 * taps + axis
-        tap_ref[at : at + 1, :] = jnp.zeros((1, 128), jnp.float32) + frac[axis]
-
-    fz = frac[0]
-    base = level[0, 0, 0].astype(jnp.float32)
-
-    @pl.loop(0, blocks // CHUNK)
-    def _(c):
-        fetch(c).wait()
-        for i in range(CHUNK):
-            b = c * CHUNK + i
-            s = dest[b]
-            o = offs[b]
-            lower = cam[b, 0] - base
-            for k in range(planes - 1):
-                upper = cam[b, k + 1] - base
-                at = pl.ds(pl.multiple_of(CZ + (o + k) * rows, 8), rows)
-                acc_ref[s, at, :] = acc_ref[s, at, :] + ((1.0 - fz) * lower + fz * upper)
-                cnt = pl.ds(o + k, 1)
-                acc_ref[s, cnt, :] = acc_ref[s, cnt, :] + 1.0
-                lower = upper
-
-
 def world_kernel(
     dims, rows, taps,
-    acc_ref, tap_in, est_ref, joined_ref,
-    ru, rd, tap_all, jx, e0, e1, kx, za, zb, rt, yb, part, lg,
-    us, ur, ds_, dr, tap_s, tap_r, loc_sem, ms, mr, los, lor, his, hir,
+    dest_in, offs_in, level_in, frac_in, psf_in, cam_ref, est_ref, joined_ref,
+    dest, offs, level, frac, psf, cam, acc_ref, tap_in, ru, rd, tap_all, jx, e0, e1, kx, za, zb, rt, yb, part, lg,
+    small, cam_sem, us, ur, ds_, dr, tap_s, tap_r, loc_sem, ms, mr, los, lor, his, hir,
     zs, zr, es, er, out_s, out_r,
 ):
+    pairs = ((dest_in, dest), (offs_in, offs), (level_in, level), (frac_in, frac), (psf_in, psf))
+    loads = [pltpu.make_async_copy(a, b, small.at[n]) for n, (a, b) in enumerate(pairs)]
+    for load in loads:
+        load.start()
+
+    def fetch(n):
+        at = pl.ds(n * BAND, BAND)
+        return pltpu.make_async_copy(cam_ref.at[:, :, at, :], cam.at[:, :, at, :], cam_sem.at[n])
+
+    for n in range(rows // BAND):
+        fetch(n).start()
+
     slabs, views, bands = dims
     strip = rows // views
     wide = strip + 2 * HALO
@@ -121,6 +78,48 @@
     for d in range(1, strips):
         greet(strip_dev(z, (me + d) % strips))
 
+    for load in loads:
+        load.wait()
+
+    blocks, planes = cam.shape[:2]
+    tall = acc_ref.shape[1]
+    lanes = 4 * blocks
+    lane = lax.broadcasted_iota(jnp.int32, (CZ, lanes), 1)
+    plane = lax.broadcasted_iota(jnp.int32, (CZ, lanes), 0)
+    block, later = lane % blocks, lane // blocks % 2
+    first = jnp.zeros((CZ, lanes), jnp.int32)
+    for b in range(blocks):
+        first = jnp.where(block == b, dest[b] * CZ + offs[b], first)
+    lands = [(first + later == plane + s * CZ).astype(jnp.float32) for s in range(slabs)]
+    for s in range(slabs):
+        hits = jnp.sum(jnp.where(lane < 2 * blocks, lands[s], 0.0), axis=1, keepdims=True)
+        acc_ref[s, 0:CZ, :] = jnp.broadcast_to(hits, (CZ, 128))
+    lands = jnp.concatenate(lands, axis=0).astype(jnp.bfloat16)
+
+    fz = frac[0]
+    base = level[0, 0, 0].astype(jnp.float32)
+    flat = cam.reshape(blocks * planes * rows, 128)
+    out = acc_ref.reshape(slabs * tall, 128)
+
+    def row_planes(r):
+        at = [flat[pl.ds(k * rows + r, blocks, stride=planes * rows), :] for k in range(planes)]
+        mixed = [(1.0 - fz) * at[k] + (fz * at[k + 1] - base) for k in range(planes - 1)]
+        top = [m.astype(jnp.bfloat16) for m in mixed]
+        rest = [(m - t.astype(jnp.float32)).astype(jnp.bfloat16) for m, t in zip(mixed, top)]
+        return jnp.concatenate(top + rest, axis=0)
+
+    @pl.loop(0, rows // BAND)
+    def _(n):
+        fetch(n).wait()
+        for j in range(0, BAND, 2):
+            r = n * BAND + j
+            both = jnp.concatenate([row_planes(r), row_planes(r + 1)], axis=1)
+            sums = jnp.dot(lands, both, preferred_element_type=jnp.float32)
+            for s in range(slabs):
+                for i in range(2):
+                    at = pl.ds(s * tall + CZ + r + i, CZ, stride=rows)
+                    out[at, :] = sums[s * CZ : (s + 1) * CZ, i * 128 : (i + 1) * 128]
+
     def clear(ref, planes, lo, hi):
         @pl.loop(planes[0], planes[1])
         def _(p):
@@ -169,6 +168,13 @@
         def _(k):
             for c in range(NCH):
                 down_copy(acc_ref, k, c).start()
+
+    for axis in range(3):
+        scale = jnp.sum(psf[axis], axis=1, keepdims=True)
+        share = psf[axis] / scale
+        for t in range(taps):
+            at = axis * taps + t
+            tap_in[at : at + 1, :] = jnp.broadcast_to(share[:, t : t + 1], (1, 128))
 
     own_tap = pltpu.make_async_copy(tap_in, tap_all.at[v], loc_sem)
     own_tap.start()
@@ -232,7 +238,7 @@
             kx[w, n, 0:128, 128:256] = (full - top.astype(jnp.float32)).astype(jnp.bfloat16)
             kx[w, n, 128:256, 128:256] = jnp.zeros((128, 128), jnp.bfloat16)
 
-    fy, fx = [tap_in[3 * taps + n : 3 * taps + n + 1, :] for n in (1, 2)]
+    fy, fx = frac[1], frac[2]
     last_row = lax.broadcasted_iota(jnp.int32, (rows, 128), 0) == rows - 1
     last_col = lax.broadcasted_iota(jnp.int32, (rows, 128), 1) == 127
     joined = joined_ref.at[0]
@@ -523,6 +529,14 @@
                 out_copy(c, w, band, idx).wait_send()
 
 
+def store_kernel(est_in, joined_in, est_out, joined_out, sems):
+    copies = [pltpu.make_async_copy(a, b, sems.at[n]) for n, (a, b) in enumerate(((est_in, est_out), (joined_in, joined_out)))]
+    for copy in copies:
+        copy.start()
+    for copy in copies:
+        copy.wait()
+
+
 def on_device(dims, camera, background, destination, offsets, shift_frac, psf_taps):
     slabs, views, bands = dims
     blocks, planes, rows, cols = camera.shape[1:]
@@ -531,38 +545,14 @@
     tall = CZ * rows + CZ
     strip = rows // views
     wide = strip + 2 * HALO
-    tap_rows = -(-3 * (taps + 1) // 8) * 8
+    tap_rows = -(-3 * taps // 8) * 8
     vmem = pl.BlockSpec(memory_space=pltpu.VMEM)
     hbm = functools.partial(pltpu.with_memory_space_constraint, memory_space=pltpu.HBM)
-    cell = 4 * cols
     room = 2 * 1024 * 1024
-    acc, tap_rows_all = pl.pallas_call(
-        functools.partial(deposit_kernel, rows),
-        in_specs=[pl.BlockSpec(memory_space=pltpu.HBM)] * 6,
-        out_specs=(vmem, vmem),
-        out_shape=(
-            pltpu.VMEM((slabs, tall, cols), jnp.float32),
-            pltpu.VMEM((tap_rows, cols), jnp.float32),
-        ),
-        scratch_shapes=[
-            pltpu.SMEM((blocks,), jnp.int32),
-            pltpu.SMEM((blocks,), jnp.int32),
-            pltpu.SMEM((1, 1, 1), jnp.int32),
-            pltpu.SMEM((3,), jnp.float32),
-            pltpu.VMEM((3, 1, taps), jnp.float32),
-            pltpu.VMEM((blocks, planes, rows, cols), jnp.float32),
-            pltpu.SemaphoreType.DMA((blocks // CHUNK,)),
-            pltpu.SemaphoreType.DMA((5,)),
-        ],
-        compiler_params=pltpu.CompilerParams(
-            vmem_limit_bytes=cell * (blocks * planes * rows + slabs * tall) + room),
-        name="deposit",
-    )(hbm(destination.reshape(-1)), hbm(offsets.reshape(-1)), background, hbm(shift_frac[0]),
-      hbm(jnp.transpose(psf_taps, (1, 0, 2))), hbm(camera[0]))
-
     dma = pltpu.SemaphoreType.DMA
     f32 = jnp.float32
     shapes = [
+        (blocks, planes, rows, cols), (slabs, tall, cols), (tap_rows, cols),
         (slabs, tall, cols), (slabs, tall, cols), (views, tap_rows, cols),
         (views, 3 * CZ, wide, cols), (3 * CZ, wide, cols), (3 * CZ, wide, cols),
     ]
@@ -572,19 +562,24 @@
         (OC, strip, cols), (views, OC, strip, cols), (CZ, strip, cols),
     ]
     total = sum([functools.reduce(lambda a, b: a * b, s) for s in shapes + late])
-    total = total + cols * (slabs * tall + 2 * CZ * rows + views * 4 * cols)
+    total = total + cols * (2 * CZ * rows + views * 4 * cols)
     estimate, joined = pl.pallas_call(
         functools.partial(world_kernel, dims, rows, taps),
-        in_specs=[vmem, vmem],
+        in_specs=[pl.BlockSpec(memory_space=pltpu.HBM)] * 6,
         out_specs=(vmem, vmem),
         out_shape=(
-            jax.ShapeDtypeStruct((CZ, rows, cols), f32),
-            jax.ShapeDtypeStruct((1, CZ, rows, cols), f32),
+            pltpu.VMEM((CZ, rows, cols), f32),
+            pltpu.VMEM((1, CZ, rows, cols), f32),
         ),
-        scratch_shapes=[pltpu.VMEM(s, f32) for s in shapes]
+        scratch_shapes=[
+            pltpu.SMEM((blocks,), jnp.int32), pltpu.SMEM((blocks,), jnp.int32),
+            pltpu.SMEM((1, 1, 1), jnp.int32), pltpu.SMEM((3,), f32), pltpu.VMEM((3, 1, taps), f32),
+        ]
+        + [pltpu.VMEM(s, f32) for s in shapes]
         + [pltpu.VMEM((views, 2, 2 * cols, 2 * cols), jnp.bfloat16)]
         + [pltpu.VMEM(s, f32) for s in late]
         + [
+            dma((5,)), dma((rows // BAND,)),
             dma((slabs, NCH)), dma((slabs, NCH)), dma((slabs, NCH)), dma((slabs, NCH)),
             dma((views,)), dma((views,)), dma,
             dma((views, NCH)), dma((views, NCH)), dma((NCH,)), dma((views, NCH)), dma((NCH,)), dma((views, NCH)),
@@ -594,8 +589,16 @@
         compiler_params=pltpu.CompilerParams(
             collective_id=0, has_side_effects=True, vmem_limit_bytes=4 * total + room),
         name="world",
-    )(acc, tap_rows_all)
-    return estimate, joined
+    )(hbm(destination.reshape(-1)), hbm(offsets.reshape(-1)), background, hbm(shift_frac[0]),
+      hbm(jnp.transpose(psf_taps, (1, 0, 2))), hbm(camera[0]))
+    return pl.pallas_call(
+        store_kernel,
+        in_specs=[vmem, vmem],
+        out_specs=(pl.BlockSpec(memory_space=pltpu.HBM), pl.BlockSpec(memory_space=pltpu.HBM)),
+        out_shape=(jax.ShapeDtypeStruct(estimate.shape, f32), jax.ShapeDtypeStruct(joined.shape, f32)),
+        scratch_shapes=[dma((2,))],
+        name="store",
+    )(pltpu.with_memory_space_constraint(estimate, pltpu.VMEM), pltpu.with_memory_space_constraint(joined, pltpu.VMEM))
 
 
 def solution(mesh):

time: 53.3 us -> 54.8 us (1.028)
  Pallas kernels: 50.4 us -> 53.3 us
  local copies, waits for them, and re-layouts: 1.41 us -> 0 us
    pallas_call x1, Pallas kernels: 48 us -> 52.5 us  [on_device(): pl.pallas_call(functools.partial(world_kernel, dims, rows, taps), in_spec...]
    pallas_call x1, Pallas kernels: 2.44 us -> 0.81 us  [on_device(): pl.pallas_call(store_kernel, in_specs=[vmem, vmem], out_specs=(pl.BlockSp...]
    unnamed x2 -> x0, local copies, waits for them, and re-layouts: 1.41 us -> none
where the time goes in v4:
time: 54.8 us; the launch traced here: 54.6 us
  Pallas kernels  53.3 us (97%)
  between operations  1.28 us (2%)
    pallas_call x1, Pallas kernels, on_device(): pl.pallas_call(functools.partial(world_kernel, dims, rows, taps), in_spec...  52.5 us

profile of v4, /device:TPU:1, one launch (start us, length us, event | category | flops | bytes accessed | tf_op | source)
XLA Modules:
  0.0 54.6 jit_solution(11864787403684682158)
XLA Ops:
  1.3 52.5 %world.1 = (f32[8,64,128]{2,1,0:T(8,128)S(1)}, f32[1,8,64,128]{3,2,1,0:T(8,128)S(1)}) custom-call(s32[32]{0:T(128)} %bitcast.7, s32[32]{0:T(128)} %bitcast.8, s32[1,1,1]{2,1,0:T(1,128)S(6)} %copy.8.level_in, f32[3]{0:T(128)} %bitcast.9, f32[3,1,9]{2,1,0:T(1,128)} %bitcast.6, f32[32,3,64,128]{3,2,1,0:T(8,128)} %bitcast.5), custom_call_target="tpu_custom_call" | custom-call | tf_op jit(solution)/shard_map/world/pallas_call | solution.py:566
  53.8 0.8 %store.1 = (f32[8,64,128]{2,1,0:T(8,128)}, f32[1,8,64,128]{3,2,1,0:T(8,128)}) custom-call(f32[8,64,128]{2,1,0:T(8,128)S(1)} %get-tuple-element.4.est_in, f32[1,8,64,128]{3,2,1,0:T(8,128)S(1)} %get-tuple-element.5.joined_in), custom_call_target="tpu_custom_call" | custom-call | tf_op jit(solution)/shard_map/store/pallas_call | solution.py:594

commit v5 on v3

--- a/solution.py
+++ b/solution.py
@@ -108,15 +108,11 @@
     def greet(target):
         pl.semaphore_signal(barrier, inc=1, device_id=target, device_id_type=MESH)
 
-    amount = strips - 1
-    for dz, zok in ((-1, below), (1, above)):
-        for ds, sok in ((-1, left), (0, z >= 0), (1, right)):
-            ok = zok & sok
-            amount = amount + ok.astype(jnp.int32)
-
-            @pl.when(ok)
-            def _(dz=dz, ds=ds):
-                greet(strip_dev(z + dz, me + ds))
+    amount = strips - 1 + below.astype(jnp.int32) + above.astype(jnp.int32)
+    for dz, ok in ((1, above), (-1, below)):
+        @pl.when(ok)
+        def _(dz=dz):
+            greet(dev(z + dz, v, g))
 
     for d in range(1, strips):
         greet(strip_dev(z, (me + d) % strips))
@@ -125,6 +121,36 @@
         @pl.loop(planes[0], planes[1])
         def _(p):
             ref[p, lo:hi, :] = jnp.zeros((hi - lo, 128), jnp.float32)
+
+    pl.semaphore_wait(barrier, amount)
+
+    def span(c):
+        start = 0 if c == 0 else CZ + c * CP * rows
+        return pl.ds(start, CZ + (c + 1) * CP * rows - start)
+
+    def up_copy(src, t, c):
+        return pltpu.make_async_remote_copy(
+            src_ref=src.at[t, span(c)], dst_ref=ru.at[t, span(c)], send_sem=us.at[t, c],
+            recv_sem=ur.at[t, c], device_id={"gz": z + 1}, device_id_type=MESH)
+
+    def down_copy(src, t, c):
+        return pltpu.make_async_remote_copy(
+            src_ref=src.at[t, span(c)], dst_ref=rd.at[t, span(c)], send_sem=ds_.at[t, c],
+            recv_sem=dr.at[t, c], device_id={"gz": z - 1}, device_id_type=MESH)
+
+    @pl.when(z == 0)
+    def _():
+        @pl.loop(0, slabs - 1)
+        def _(k):
+            for c in range(NCH):
+                up_copy(acc_ref, slabs - 1 - k, c).start()
+
+    @pl.when(z == slabs - 1)
+    def _():
+        @pl.loop(0, slabs - 1)
+        def _(k):
+            for c in range(NCH):
+                down_copy(acc_ref, k, c).start()
 
     for edge, flow, halo in ((z == 0, ru, (0, CZ)), (z == slabs - 1, rd, (2 * CZ, 3 * CZ))):
         @pl.when(edge)
@@ -139,36 +165,6 @@
             clear(e1, (0, 3 * CZ), lo, hi)
             for w in range(views):
                 clear(jx.at[w], (CZ, 2 * CZ), lo, hi)
-
-    pl.semaphore_wait(barrier, amount)
-
-    def span(c):
-        start = 0 if c == 0 else CZ + c * CP * rows
-        return pl.ds(start, CZ + (c + 1) * CP * rows - start)
-
-    def up_copy(src, t, c):
-        return pltpu.make_async_remote_copy(
-            src_ref=src.at[t, span(c)], dst_ref=ru.at[t, span(c)], send_sem=us.at[t, c],
-            recv_sem=ur.at[t, c], device_id={"gz": z + 1}, device_id_type=MESH)
-
-    def down_copy(src, t, c):
-        return pltpu.make_async_remote_copy(
-            src_ref=src.at[t, span(c)], dst_ref=rd.at[t, span(c)], send_sem=ds_.at[t, c],
-            recv_sem=dr.at[t, c], device_id={"gz": z - 1}, device_id_type=MESH)
-
-    @pl.when(z == 0)
-    def _():
-        @pl.loop(0, slabs - 1)
-        def _(k):
-            for c in range(NCH):
-                up_copy(acc_ref, slabs - 1 - k, c).start()
-
-    @pl.when(z == slabs - 1)
-    def _():
-        @pl.loop(0, slabs - 1)
-        def _(k):
-            for c in range(NCH):
-                down_copy(acc_ref, k, c).start()
 
     own_tap = pltpu.make_async_copy(tap_in, tap_all.at[v], loc_sem)
     own_tap.start()
@@ -521,6 +517,14 @@
             @pl.when((w != v) | (band != g))
             def _(w=w, c=c):
                 out_copy(c, w, band, idx).wait_send()
+
+
+def store_kernel(est_in, joined_in, est_out, joined_out, sems):
+    copies = [pltpu.make_async_copy(a, b, sems.at[n]) for n, (a, b) in enumerate(((est_in, est_out), (joined_in, joined_out)))]
+    for copy in copies:
+        copy.start()
+    for copy in copies:
+        copy.wait()
 
 
 def on_device(dims, camera, background, destination, offsets, shift_frac, psf_taps):
@@ -578,8 +582,8 @@
         in_specs=[vmem, vmem],
         out_specs=(vmem, vmem),
         out_shape=(
-            jax.ShapeDtypeStruct((CZ, rows, cols), f32),
-            jax.ShapeDtypeStruct((1, CZ, rows, cols), f32),
+            pltpu.VMEM((CZ, rows, cols), f32),
+            pltpu.VMEM((1, CZ, rows, cols), f32),
         ),
         scratch_shapes=[pltpu.VMEM(s, f32) for s in shapes]
         + [pltpu.VMEM((views, 2, 2 * cols, 2 * cols), jnp.bfloat16)]
@@ -595,7 +599,14 @@
             collective_id=0, has_side_effects=True, vmem_limit_bytes=4 * total + room),
         name="world",
     )(acc, tap_rows_all)
-    return estimate, joined
+    return pl.pallas_call(
+        store_kernel,
+        in_specs=[vmem, vmem],
+        out_specs=(pl.BlockSpec(memory_space=pltpu.HBM), pl.BlockSpec(memory_space=pltpu.HBM)),
+        out_shape=(jax.ShapeDtypeStruct(estimate.shape, f32), jax.ShapeDtypeStruct(joined.shape, f32)),
+        scratch_shapes=[dma((2,))],
+        name="store",
+    )(pltpu.with_memory_space_constraint(estimate, pltpu.VMEM), pltpu.with_memory_space_constraint(joined, pltpu.VMEM))
 
 
 def solution(mesh):

time: 53.3 us -> 53 us (level)
  local copies, waits for them, and re-layouts: 1.41 us -> 0 us
  Pallas kernels: 50.4 us -> 51.6 us
    unnamed x2 -> x0, local copies, waits for them, and re-layouts: 1.41 us -> none
    pallas_call x0 -> x1, Pallas kernels: none -> 0.81 us  [on_device(): pl.pallas_call(store_kernel, in_specs=[vmem, vmem], out_specs=(pl.BlockSp...]
where the time goes in v5:
time: 53 us; the launch traced here: 52.9 us
  Pallas kernels  51.6 us (97%)
  between operations  1.29 us (2%)
    pallas_call x1, Pallas kernels, on_device(): pl.pallas_call(functools.partial(world_kernel, dims, rows, taps), in_spec...  48.3 us
    pallas_call x1, Pallas kernels, on_device(): pl.pallas_call(functools.partial(deposit_kernel, rows), in_specs=[pl.Bloc...  2.45 us

profile of v5, /device:TPU:1, one launch (start us, length us, event | category | flops | bytes accessed | tf_op | source)
XLA Modules:
  0.0 52.9 jit_solution(14530278310908150282)
XLA Ops:
  1.3 2.4 %deposit.1 = (f32[4,520,128]{2,1,0:T(8,128)S(1)}, f32[32,128]{1,0:T(8,128)S(1)}) custom-call(s32[32]{0:T(128)} %bitcast.7, s32[32]{0:T(128)} %bitcast.8, s32[1,1,1]{2,1,0:T(1,128)S(6)} %copy.8.level_in, f32[3]{0:T(128)} %bitcast.9, f32[3,1,9]{2,1,0:T(1,128)} %bitcast.6, f32[32,3,64,128]{3,2,1,0:T(8,128)} %bitcast.5), custom_call_target="tpu_custom_call" | custom-call | tf_op jit(solution)/shard_map/deposit/pallas_call | solution.py:543
  3.7 48.3 %world.1 = (f32[8,64,128]{2,1,0:T(8,128)S(1)}, f32[1,8,64,128]{3,2,1,0:T(8,128)S(1)}) custom-call(f32[4,520,128]{2,1,0:T(8,128)S(1)} %get-tuple-element.6.acc_ref, f32[32,128]{1,0:T(8,128)S(1)} %get-tuple-element.7.tap_in), custom_call_target="tpu_custom_call" | custom-call | tf_op jit(solution)/shard_map/world/pallas_call | solution.py:580
  52.0 0.8 %store.1 = (f32[8,64,128]{2,1,0:T(8,128)}, f32[1,8,64,128]{3,2,1,0:T(8,128)}) custom-call(f32[8,64,128]{2,1,0:T(8,128)S(1)} %get-tuple-element.8.est_in, f32[1,8,64,128]{3,2,1,0:T(8,128)S(1)} %get-tuple-element.9.joined_in), custom_call_target="tpu_custom_call" | custom-call | tf_op jit(solution)/shard_map/store/pallas_call | solution.py:602

commit v6 on v5

--- a/solution.py
+++ b/solution.py
@@ -79,7 +79,7 @@
 def world_kernel(
     dims, rows, taps,
     acc_ref, tap_in, est_ref, joined_ref,
-    ru, rd, tap_all, jx, e0, e1, kx, za, zb, rt, yb, part, lg,
+    ru, rd, tap_all, jx, e0, e1, kx, xb, za, zb, yb, lg,
     us, ur, ds_, dr, tap_s, tap_r, loc_sem, ms, mr, los, lor, his, hir,
     zs, zr, es, er, out_s, out_r,
 ):
@@ -336,23 +336,6 @@
                 for copy in z_copies(c, up):
                     copy.start()
 
-    join(0)
-    for c in range(1, NCH):
-        join(c)
-        spread(c - 1)
-    spread(NCH - 1)
-
-    for c in range(NCH):
-        for up, ok in ((True, below), (False, above)):
-            @pl.when(ok)
-            def _(up=up, c=c):
-                copies = z_copies(c, up)
-                for copy in copies:
-                    copy.wait_recv()
-                if len(copies) == views and views > 1:
-                    for p in range(c * CP, (c + 1) * CP):
-                        average((0 if up else 2 * CZ) + p)
-
     planes_r = CZ + 2 * margin
     rows_r = strip + 2 * margin
 
@@ -378,50 +361,66 @@
             return jnp.exp(total / len(terms))
         return root([jnp.sqrt(a * b) for a, b in zip(terms[0::2], terms[1::2])])
 
+    def tap(w, axis, t):
+        at = axis * taps + t
+        return tap_all[w, at : at + 1, :]
+
+    def blur_rows(est, first):
+        for p in range(OC):
+            terms = [est[first + p, t : t + rows_r, :] for t in range(taps)]
+            for w in range(views):
+                zb[w, p] = weighted(terms, [tap(w, 1, t) for t in range(taps)])
+        for w in range(views):
+            xb[w, pl.ds(first, OC)] = along_x(zb[w].reshape(OC * rows_r, 128), w, 0).reshape(OC, rows_r, 128)
+
     def correct(est, emit):
-        for w in range(views):
-            def tap(axis, t, w=w):
-                at = axis * taps + t
-                return tap_all[w, at : at + 1, :]
-
-            @pl.loop(0, wide // 8, unroll=2)
-            def _(r):
-                at = pl.ds(pl.multiple_of(r * 8, 8), 8)
-                column = [est[CZ - 2 * margin + p, at, :] for p in range(planes_r + 2 * margin)]
+        @pl.loop(0, rows_r // 8)
+        def _(r):
+            at = pl.ds(pl.multiple_of(r * 8, 8), 8)
+            for w in range(views):
+                column = [xb[w, p, at, :] for p in range(3 * CZ)]
+                ratio = []
                 for p in range(planes_r):
-                    za[p, at, :] = weighted(column[p : p + taps], [tap(0, t) for t in range(taps)])
-
-            @pl.loop(0, planes_r, unroll=4)
-            def _(p):
-                base = HALO - 2 * margin
-                zb[p] = weighted([za[p, base + t : base + t + rows_r, :] for t in range(taps)],
-                                 [tap(1, t) for t in range(taps)])
-
-            @pl.loop(0, planes_r // 4)
-            def _(c):
-                at = pl.ds(c * 4, 4)
-                blurred = along_x(zb[at].reshape(4 * rows_r, 128), w, 0).reshape(4, rows_r, 128)
-                data = jx[w, pl.ds(c * 4 + CZ - margin, 4), HALO - margin : HALO - margin + rows_r, :]
-                blurred = jnp.maximum(blurred, TINY)
-                inverse = pl.reciprocal(blurred, approx=True)
-                inverse = inverse * (2.0 - blurred * inverse)
-                rt[w, at] = data * inverse
+                    first = CZ - 2 * margin + p
+                    blurred = weighted(column[first : first + taps], [tap(w, 0, t) for t in range(taps)])
+                    blurred = jnp.maximum(blurred, TINY)
+                    inverse = pl.reciprocal(blurred, approx=True)
+                    inverse = inverse * (2.0 - blurred * inverse)
+                    ratio.append(jx[w, CZ - margin + p, pl.ds(r * 8 + HALO - margin, 8), :] * inverse)
+                for p in range(CZ):
+                    za[w, p, at, :] = weighted(ratio[p : p + taps], [tap(w, 0, taps - 1 - t) for t in range(taps)])
 
         for c in range(NOUT):
+            factors = []
             for w in range(views):
-                def tap(axis, t, w=w):
-                    at = axis * taps + taps - 1 - t
-                    return tap_all[w, at : at + 1, :]
-
-                for r in range(rows_r // 8):
-                    at = pl.ds(r * 8, 8)
-                    column = [rt[w, c * OC + p, at, :] for p in range(OC + 2 * margin)]
-                    for p in range(OC):
-                        za[p, at, :] = weighted(column[p : p + taps], [tap(0, t) for t in range(taps)])
                 for p in range(OC):
-                    yb[p] = weighted([za[p, t : t + strip, :] for t in range(taps)], [tap(1, t) for t in range(taps)])
-                part[w] = along_x(yb[...].reshape(OC * strip, 128), w, 1).reshape(OC, strip, 128)
-            emit(c, est[pl.ds(CZ + c * OC, OC), HALO : HALO + strip, :] * root([part[w] for w in range(views)]))
+                    yb[w, p] = weighted([za[w, c * OC + p, t : t + strip, :] for t in range(taps)],
+                                        [tap(w, 1, taps - 1 - t) for t in range(taps)])
+                factors.append(along_x(yb[w].reshape(OC * strip, 128), w, 1).reshape(OC, strip, 128))
+            emit(c, est[pl.ds(CZ + c * OC, OC), HALO : HALO + strip, :] * root(factors))
+
+    join(0)
+    for c in range(1, NCH):
+        join(c)
+        spread(c - 1)
+    for c in range(NOUT - 1):
+        blur_rows(e0, CZ + c * OC)
+    spread(NCH - 1)
+    blur_rows(e0, 2 * CZ - OC)
+
+    for group in range(NOUT):
+        for up, ok in ((True, below), (False, above)):
+            @pl.when(ok)
+            def _(up=up, group=group):
+                for c in range(group * OC // CP, (group + 1) * OC // CP):
+                    copies = z_copies(c, up)
+                    for copy in copies:
+                        copy.wait_recv()
+                    if len(copies) == views and views > 1:
+                        for p in range(c * CP, (c + 1) * CP):
+                            average((0 if up else 2 * CZ) + p)
+
+            blur_rows(e0, (0 if up else 2 * CZ) + group * OC)
 
     inner = pl.ds(HALO, strip)
     near = []
@@ -472,11 +471,20 @@
                 for copy in z_copies(c, up):
                     copy.wait_send()
 
+    def near_wait(c, way):
+        for n, dz, ds, _, ok in near:
+            if dz == way:
+                @pl.when(ok)
+                def _(n=n, dz=dz, ds=ds):
+                    near_copy(n, dz, ds, c).wait_recv()
+
     for c in range(NOUT):
-        for n, dz, ds, _, ok in near:
-            @pl.when(ok)
-            def _(n=n, dz=dz, ds=ds, c=c):
-                near_copy(n, dz, ds, c).wait_recv()
+        near_wait(c, 0)
+        blur_rows(e1, CZ + c * OC)
+    for c in range(NOUT):
+        for way in (1, -1):
+            near_wait(c, way)
+            blur_rows(e1, CZ - way * CZ + c * OC)
 
     def out_copy(c, w, target_g, i):
         at = pl.ds(pl.multiple_of(i * strip, 8), strip)
@@ -571,9 +579,8 @@
         (views, 3 * CZ, wide, cols), (3 * CZ, wide, cols), (3 * CZ, wide, cols),
     ]
     late = [
-        (CZ + 2 * margin, wide, cols),
-        (CZ + 2 * margin, strip + 2 * margin, cols), (views, CZ + 2 * margin, strip + 2 * margin, cols),
-        (OC, strip, cols), (views, OC, strip, cols), (CZ, strip, cols),
+        (views, 3 * CZ, strip + 2 * margin, cols), (views, CZ, strip + 2 * margin, cols),
+        (views, OC, strip + 2 * margin, cols), (views, OC, strip, cols), (CZ, strip, cols),
     ]
     total = sum([functools.reduce(lambda a, b: a * b, s) for s in shapes + late])
     total = total + cols * (slabs * tall + 2 * CZ * rows + views * 4 * cols)

time: 53 us -> 49.9 us (0.942)
  Pallas kernels: 51.6 us -> 48.4 us
    pallas_call x1, Pallas kernels: 48.3 us -> 45.2 us  [on_device(): pl.pallas_call(functools.partial(world_kernel, dims, rows, taps), in_spec...]
where the time goes in v6:
time: 49.9 us; the launch traced here: 49.7 us
  Pallas kernels  48.4 us (97%)
  between operations  1.29 us (3%)
    pallas_call x1, Pallas kernels, on_device(): pl.pallas_call(functools.partial(world_kernel, dims, rows, taps), in_spec...  45.2 us
    pallas_call x1, Pallas kernels, on_device(): pl.pallas_call(functools.partial(deposit_kernel, rows), in_specs=[pl.Bloc...  2.44 us

profile of v6, /device:TPU:1, one launch (start us, length us, event | category | flops | bytes accessed | tf_op | source)
XLA Modules:
  0.0 49.7 jit_solution(15121590842631056725)
XLA Ops:
  1.3 2.4 %deposit.1 = (f32[4,520,128]{2,1,0:T(8,128)S(1)}, f32[32,128]{1,0:T(8,128)S(1)}) custom-call(s32[32]{0:T(128)} %bitcast.7, s32[32]{0:T(128)} %bitcast.8, s32[1,1,1]{2,1,0:T(1,128)S(6)} %copy.8.level_in, f32[3]{0:T(128)} %bitcast.9, f32[3,1,9]{2,1,0:T(1,128)} %bitcast.6, f32[32,3,64,128]{3,2,1,0:T(8,128)} %bitcast.5), custom_call_target="tpu_custom_call" | custom-call | tf_op jit(solution)/shard_map/deposit/pallas_call | solution.py:551
  3.7 45.2 %world.1 = (f32[8,64,128]{2,1,0:T(8,128)S(1)}, f32[1,8,64,128]{3,2,1,0:T(8,128)S(1)}) custom-call(f32[4,520,128]{2,1,0:T(8,128)S(1)} %get-tuple-element.6.acc_ref, f32[32,128]{1,0:T(8,128)S(1)} %get-tuple-element.7.tap_in), custom_call_target="tpu_custom_call" | custom-call | tf_op jit(solution)/shard_map/world/pallas_call | solution.py:587
  48.9 0.8 %store.1 = (f32[8,64,128]{2,1,0:T(8,128)}, f32[1,8,64,128]{3,2,1,0:T(8,128)}) custom-call(f32[8,64,128]{2,1,0:T(8,128)S(1)} %get-tuple-element.8.est_in, f32[1,8,64,128]{3,2,1,0:T(8,128)S(1)} %get-tuple-element.9.joined_in), custom_call_target="tpu_custom_call" | custom-call | tf_op jit(solution)/shard_map/store/pallas_call | solution.py:609

commit v7 on v6

--- a/solution.py
+++ b/solution.py
@@ -22,12 +22,12 @@
 
 
 def deposit_kernel(
-    rows, dest_in, offs_in, level_in, frac_in, psf_in, cam_ref, acc_ref, tap_ref,
-    dest, offs, level, frac, psf, cam, sems, small,
+    rows, dest_in, offs_in, level_in, frac_in, cam_ref, acc_ref,
+    dest, offs, level, frac, hits, cam, sems, small,
 ):
-    taps = psf.shape[2]
     blocks, planes = cam_ref.shape[:2]
-    pairs = ((dest_in, dest), (offs_in, offs), (level_in, level), (frac_in, frac), (psf_in, psf))
+    slabs = acc_ref.shape[0]
+    pairs = ((dest_in, dest), (offs_in, offs), (level_in, level), (frac_in, frac))
     copies = [pltpu.make_async_copy(a, b, small.at[n]) for n, (a, b) in enumerate(pairs)]
     for copy in copies:
         copy.start()
@@ -39,22 +39,14 @@
     for c in range(blocks // CHUNK):
         fetch(c).start()
 
-    @pl.loop(0, acc_ref.shape[0])
+    @pl.loop(0, slabs)
     def _(s):
+        for p in range(CZ):
+            hits[s * CZ + p] = 0
         acc_ref[s] = jnp.zeros(acc_ref.shape[1:], jnp.float32)
 
     for copy in copies:
         copy.wait()
-
-    tap_ref[...] = jnp.zeros(tap_ref.shape, jnp.float32)
-    for axis in range(3):
-        scale = jnp.sum(psf[axis], axis=1, keepdims=True)
-        share = psf[axis] / scale
-        for t in range(taps):
-            at = axis * taps + t
-            tap_ref[at : at + 1, :] = jnp.broadcast_to(share[:, t : t + 1], (1, 128))
-        at = 3 * taps + axis
-        tap_ref[at : at + 1, :] = jnp.zeros((1, 128), jnp.float32) + frac[axis]
 
     fz = frac[0]
     base = level[0, 0, 0].astype(jnp.float32)
@@ -66,23 +58,29 @@
             b = c * CHUNK + i
             s = dest[b]
             o = offs[b]
-            lower = cam[b, 0] - base
+            mixed = (1.0 - fz) * cam[b, 0 : planes - 1] + (fz * cam[b, 1:planes] - base)
+            at = pl.ds(pl.multiple_of(CZ + o * rows, 8), (planes - 1) * rows)
+            acc_ref[s, at, :] = acc_ref[s, at, :] + mixed.reshape((planes - 1) * rows, 128)
             for k in range(planes - 1):
-                upper = cam[b, k + 1] - base
-                at = pl.ds(pl.multiple_of(CZ + (o + k) * rows, 8), rows)
-                acc_ref[s, at, :] = acc_ref[s, at, :] + ((1.0 - fz) * lower + fz * upper)
-                cnt = pl.ds(o + k, 1)
-                acc_ref[s, cnt, :] = acc_ref[s, cnt, :] + 1.0
-                lower = upper
+                hits[s * CZ + o + k] = hits[s * CZ + o + k] + 1
+
+    @pl.loop(0, slabs, unroll=4)
+    def _(s):
+        for p in range(CZ):
+            acc_ref[s, p : p + 1, :] = jnp.zeros((1, 128), jnp.float32) + hits[s * CZ + p].astype(jnp.float32)
 
 
 def world_kernel(
     dims, rows, taps,
-    acc_ref, tap_in, est_ref, joined_ref,
-    ru, rd, tap_all, jx, e0, e1, kx, xb, za, zb, yb, lg,
-    us, ur, ds_, dr, tap_s, tap_r, loc_sem, ms, mr, los, lor, his, hir,
+    acc_ref, frac_in, psf_in, est_ref, joined_ref,
+    frac, psf, tap_in, ru, rd, tap_all, jx, e0, e1, kx, xb, rt, za, zb, yb, lg,
+    small, us, ur, ds_, dr, tap_s, tap_r, loc_sem, ms, mr, los, lor, his, hir,
     zs, zr, es, er, out_s, out_r,
 ):
+    loads = [pltpu.make_async_copy(a, b, small.at[n]) for n, (a, b) in enumerate(((frac_in, frac), (psf_in, psf)))]
+    for load in loads:
+        load.start()
+
     slabs, views, bands = dims
     strip = rows // views
     wide = strip + 2 * HALO
@@ -165,6 +163,16 @@
             clear(e1, (0, 3 * CZ), lo, hi)
             for w in range(views):
                 clear(jx.at[w], (CZ, 2 * CZ), lo, hi)
+
+    for load in loads:
+        load.wait()
+
+    for axis in range(3):
+        scale = jnp.sum(psf[axis], axis=1, keepdims=True)
+        share = psf[axis] / scale
+        for t in range(taps):
+            at = axis * taps + t
+            tap_in[at : at + 1, :] = jnp.broadcast_to(share[:, t : t + 1], (1, 128))
 
     own_tap = pltpu.make_async_copy(tap_in, tap_all.at[v], loc_sem)
     own_tap.start()
@@ -228,7 +236,7 @@
             kx[w, n, 0:128, 128:256] = (full - top.astype(jnp.float32)).astype(jnp.bfloat16)
             kx[w, n, 128:256, 128:256] = jnp.zeros((128, 128), jnp.bfloat16)
 
-    fy, fx = [tap_in[3 * taps + n : 3 * taps + n + 1, :] for n in (1, 2)]
+    fy, fx = frac[1], frac[2]
     last_row = lax.broadcasted_iota(jnp.int32, (rows, 128), 0) == rows - 1
     last_col = lax.broadcasted_iota(jnp.int32, (rows, 128), 1) == 127
     joined = joined_ref.at[0]
@@ -373,28 +381,39 @@
         for w in range(views):
             xb[w, pl.ds(first, OC)] = along_x(zb[w].reshape(OC * rows_r, 128), w, 0).reshape(OC, rows_r, 128)
 
+    def ratios(r, at, w, lo, hi):
+        base = CZ - 2 * margin
+        column = [xb[w, base + p, at, :] for p in range(lo, hi + 2 * margin)]
+        out = []
+        for p in range(lo, hi):
+            blurred = weighted(column[p - lo : p - lo + taps], [tap(w, 0, t) for t in range(taps)])
+            blurred = jnp.maximum(blurred, TINY)
+            inverse = pl.reciprocal(blurred, approx=True)
+            inverse = inverse * (2.0 - blurred * inverse)
+            out.append(jx[w, CZ - margin + p, pl.ds(r * 8 + HALO - margin, 8), :] * inverse)
+        return out
+
     def correct(est, emit):
-        @pl.loop(0, rows_r // 8)
-        def _(r):
-            at = pl.ds(pl.multiple_of(r * 8, 8), 8)
-            for w in range(views):
-                column = [xb[w, p, at, :] for p in range(3 * CZ)]
-                ratio = []
-                for p in range(planes_r):
-                    first = CZ - 2 * margin + p
-                    blurred = weighted(column[first : first + taps], [tap(w, 0, t) for t in range(taps)])
-                    blurred = jnp.maximum(blurred, TINY)
-                    inverse = pl.reciprocal(blurred, approx=True)
-                    inverse = inverse * (2.0 - blurred * inverse)
-                    ratio.append(jx[w, CZ - margin + p, pl.ds(r * 8 + HALO - margin, 8), :] * inverse)
-                for p in range(CZ):
-                    za[w, p, at, :] = weighted(ratio[p : p + taps], [tap(w, 0, taps - 1 - t) for t in range(taps)])
-
         for c in range(NOUT):
+            done = c * OC + 2 * margin if c > 0 else 0
+            stop = (c + 1) * OC + 2 * margin
+
+            @pl.loop(0, rows_r // 8, unroll=True)
+            def _(r, c=c, done=done, stop=stop):
+                at = pl.ds(pl.multiple_of(r * 8, 8), 8)
+                for w in range(views):
+                    ratio = [rt[w, p, at, :] for p in range(c * OC, done)] + ratios(r, at, w, done, stop)
+                    if c < NOUT - 1:
+                        for p in range((c + 1) * OC, stop):
+                            if p >= done:
+                                rt[w, p, at, :] = ratio[p - c * OC]
+                    for p in range(OC):
+                        za[w, p, at, :] = weighted(ratio[p : p + taps], [tap(w, 0, taps - 1 - t) for t in range(taps)])
+
             factors = []
             for w in range(views):
                 for p in range(OC):
-                    yb[w, p] = weighted([za[w, c * OC + p, t : t + strip, :] for t in range(taps)],
+                    yb[w, p] = weighted([za[w, p, t : t + strip, :] for t in range(taps)],
                                         [tap(w, 1, taps - 1 - t) for t in range(taps)])
                 factors.append(along_x(yb[w].reshape(OC * strip, 128), w, 1).reshape(OC, strip, 128))
             emit(c, est[pl.ds(CZ + c * OC, OC), HALO : HALO + strip, :] * root(factors))
@@ -543,34 +562,32 @@
     tall = CZ * rows + CZ
     strip = rows // views
     wide = strip + 2 * HALO
-    tap_rows = -(-3 * (taps + 1) // 8) * 8
+    tap_rows = -(-3 * taps // 8) * 8
     vmem = pl.BlockSpec(memory_space=pltpu.VMEM)
     hbm = functools.partial(pltpu.with_memory_space_constraint, memory_space=pltpu.HBM)
     cell = 4 * cols
     room = 2 * 1024 * 1024
-    acc, tap_rows_all = pl.pallas_call(
+    any_hbm = pl.BlockSpec(memory_space=pltpu.HBM)
+    frac, psf = hbm(shift_frac[0]), hbm(jnp.transpose(psf_taps, (1, 0, 2)))
+    acc = pl.pallas_call(
         functools.partial(deposit_kernel, rows),
-        in_specs=[pl.BlockSpec(memory_space=pltpu.HBM)] * 6,
-        out_specs=(vmem, vmem),
-        out_shape=(
-            pltpu.VMEM((slabs, tall, cols), jnp.float32),
-            pltpu.VMEM((tap_rows, cols), jnp.float32),
-        ),
+        in_specs=[any_hbm] * 5,
+        out_specs=vmem,
+        out_shape=pltpu.VMEM((slabs, tall, cols), jnp.float32),
         scratch_shapes=[
             pltpu.SMEM((blocks,), jnp.int32),
             pltpu.SMEM((blocks,), jnp.int32),
             pltpu.SMEM((1, 1, 1), jnp.int32),
             pltpu.SMEM((3,), jnp.float32),
-            pltpu.VMEM((3, 1, taps), jnp.float32),
+            pltpu.SMEM((slabs * CZ,), jnp.int32),
             pltpu.VMEM((blocks, planes, rows, cols), jnp.float32),
             pltpu.SemaphoreType.DMA((blocks // CHUNK,)),
-            pltpu.SemaphoreType.DMA((5,)),
+            pltpu.SemaphoreType.DMA((4,)),
         ],
         compiler_params=pltpu.CompilerParams(
             vmem_limit_bytes=cell * (blocks * planes * rows + slabs * tall) + room),
         name="deposit",
-    )(hbm(destination.reshape(-1)), hbm(offsets.reshape(-1)), background, hbm(shift_frac[0]),
-      hbm(jnp.transpose(psf_taps, (1, 0, 2))), hbm(camera[0]))
+    )(hbm(destination.reshape(-1)), hbm(offsets.reshape(-1)), background, frac, hbm(camera[0]))
 
     dma = pltpu.SemaphoreType.DMA
     f32 = jnp.float32
@@ -579,24 +596,26 @@
         (views, 3 * CZ, wide, cols), (3 * CZ, wide, cols), (3 * CZ, wide, cols),
     ]
     late = [
-        (views, 3 * CZ, strip + 2 * margin, cols), (views, CZ, strip + 2 * margin, cols),
+        (views, 3 * CZ, strip + 2 * margin, cols), (views, CZ + 2 * margin, strip + 2 * margin, cols),
+        (views, OC, strip + 2 * margin, cols),
         (views, OC, strip + 2 * margin, cols), (views, OC, strip, cols), (CZ, strip, cols),
     ]
     total = sum([functools.reduce(lambda a, b: a * b, s) for s in shapes + late])
     total = total + cols * (slabs * tall + 2 * CZ * rows + views * 4 * cols)
     estimate, joined = pl.pallas_call(
         functools.partial(world_kernel, dims, rows, taps),
-        in_specs=[vmem, vmem],
+        in_specs=[vmem, any_hbm, any_hbm],
         out_specs=(vmem, vmem),
         out_shape=(
             pltpu.VMEM((CZ, rows, cols), f32),
             pltpu.VMEM((1, CZ, rows, cols), f32),
         ),
-        scratch_shapes=[pltpu.VMEM(s, f32) for s in shapes]
+        scratch_shapes=[pltpu.SMEM((3,), f32), pltpu.VMEM((3, 1, taps), f32), pltpu.VMEM((tap_rows, cols), f32)]
+        + [pltpu.VMEM(s, f32) for s in shapes]
         + [pltpu.VMEM((views, 2, 2 * cols, 2 * cols), jnp.bfloat16)]
         + [pltpu.VMEM(s, f32) for s in late]
         + [
-            dma((slabs, NCH)), dma((slabs, NCH)), dma((slabs, NCH)), dma((slabs, NCH)),
+            dma((2,)), dma((slabs, NCH)), dma((slabs, NCH)), dma((slabs, NCH)), dma((slabs, NCH)),
             dma((views,)), dma((views,)), dma,
             dma((views, NCH)), dma((views, NCH)), dma((NCH,)), dma((views, NCH)), dma((NCH,)), dma((views, NCH)),
             dma((2, views, NCH)), dma((2, views, NCH)), dma((8, NOUT)), dma((8, NOUT)),
@@ -605,7 +624,7 @@
         compiler_params=pltpu.CompilerParams(
             collective_id=0, has_side_effects=True, vmem_limit_bytes=4 * total + room),
         name="world",
-    )(acc, tap_rows_all)
+    )(acc, frac, psf)
     return pl.pallas_call(
         store_kernel,
         in_specs=[vmem, vmem],

time: 49.9 us -> 48.8 us (0.978)
  Pallas kernels: 48.4 us -> 47.3 us
    pallas_call x1, Pallas kernels: 45.2 us -> 44.5 us  [on_device(): pl.pallas_call(functools.partial(world_kernel, dims, rows, taps), in_spec...]
where the time goes in v7:
time: 48.8 us; the launch traced here: 48.6 us
  Pallas kernels  47.3 us (97%)
  between operations  1.29 us (3%)
    pallas_call x1, Pallas kernels, on_device(): pl.pallas_call(functools.partial(world_kernel, dims, rows, taps), in_spec...  44.5 us
    pallas_call x1, Pallas kernels, on_device(): pl.pallas_call(functools.partial(deposit_kernel, rows), in_specs=[any_hbm...  1.99 us

profile of v7, /device:TPU:1, one launch (start us, length us, event | category | flops | bytes accessed | tf_op | source)
XLA Modules:
  0.0 48.6 jit_solution(14062265121311189243)
XLA Ops:
  1.3 2.0 %deposit.1.acc_ref = f32[4,520,128]{2,1,0:T(8,128)S(1)} custom-call(s32[32]{0:T(128)} %bitcast.9, s32[32]{0:T(128)} %bitcast.10, s32[1,1,1]{2,1,0:T(1,128)S(6)} %copy.8.level_in, f32[3]{0:T(128)} %bitcast.6, f32[32,3,64,128]{3,2,1,0:T(8,128)} %bitcast.5), custom_call_target="tpu_custom_call" | custom-call | tf_op jit(solution)/shard_map/deposit/pallas_call | solution.py:572
  3.3 44.5 %world.1 = (f32[8,64,128]{2,1,0:T(8,128)S(1)}, f32[1,8,64,128]{3,2,1,0:T(8,128)S(1)}) custom-call(f32[4,520,128]{2,1,0:T(8,128)S(1)} %deposit.1.acc_ref, f32[3]{0:T(128)} %bitcast.7, f32[3,1,9]{2,1,0:T(1,128)} %bitcast.8), custom_call_target="tpu_custom_call" | custom-call | tf_op jit(solution)/shard_map/world/pallas_call | solution.py:605
  47.8 0.8 %store.1 = (f32[8,64,128]{2,1,0:T(8,128)}, f32[1,8,64,128]{3,2,1,0:T(8,128)}) custom-call(f32[8,64,128]{2,1,0:T(8,128)S(1)} %get-tuple-element.4.est_in, f32[1,8,64,128]{3,2,1,0:T(8,128)S(1)} %get-tuple-element.5.joined_in), custom_call_target="tpu_custom_call" | custom-call | tf_op jit(solution)/shard_map/store/pallas_call | solution.py:628

commit v8 on v7

--- a/solution.py
+++ b/solution.py
@@ -13,8 +13,9 @@
 CHUNK = 4
 CP = 2
 NCH = CZ // CP
-OC = 4
-NOUT = CZ // OC
+CUTS = (0, 4, CZ)
+NOUT = len(CUTS) - 1
+MOST = max([b - a for a, b in zip(CUTS, CUTS[1:])])
 
 DATA_FLOOR = 0.25
 TINY = 1e-30
@@ -90,13 +91,18 @@
     g = lax.axis_index("gy")
     strips = views * bands
     me = v * bands + g
-    band, idx = me // views, me % views
+    band, idx = lax.div(me, views), lax.rem(me, views)
 
     def dev(zz, vv, gg):
         return {"gz": zz, "view": vv, "gy": gg}
 
-    def strip_dev(zz, ss):
-        return dev(zz, ss // bands, ss % bands)
+    def place(ss):
+        return lax.div(ss, bands), lax.rem(ss, bands)
+
+    around = {ds: place(jnp.clip(me + ds, 0, strips - 1)) for ds in (-1, 0, 1)}
+    in_band = [g * views + i for i in range(views)]
+    band_sides = (jnp.minimum((g + 1) * views, strips - 1), jnp.maximum(g * views - 1, 0))
+    seats = [place(t) for t in in_band + list(band_sides)]
 
     below, above = z > 0, z < slabs - 1
     left, right = me > 0, me < strips - 1
@@ -112,8 +118,10 @@
         def _(dz=dz):
             greet(dev(z + dz, v, g))
 
-    for d in range(1, strips):
-        greet(strip_dev(z, (me + d) % strips))
+    for t in range(strips):
+        @pl.when(t != me)
+        def _(t=t):
+            greet(dev(z, t // bands, t % bands))
 
     def clear(ref, planes, lo, hi):
         @pl.loop(planes[0], planes[1])
@@ -252,19 +260,19 @@
     low_edge = ((rows - HALO, rows), (0, HALO))
     high_edge = ((0, HALO), (HALO + strip, wide))
 
-    def part_copy(c, w, rows_of, target, send, recv):
+    def part_copy(c, w, rows_of, seat, send, recv):
         src_p, dst_p = planes_of(c)
         (lo, hi), (dlo, dhi) = rows_of
         return pltpu.make_async_remote_copy(
             src_ref=joined.at[src_p, pl.ds(lo, hi - lo), :], dst_ref=jx.at[w, dst_p, pl.ds(dlo, dhi - dlo), :],
-            send_sem=send, recv_sem=recv, device_id=strip_dev(z, target), device_id_type=MESH)
+            send_sem=send, recv_sem=recv, device_id=dev(z, *seat), device_id_type=MESH)
 
     def sends(c):
         out = []
         for i in range(views):
-            out.append((g * views + i, z >= 0, piece(i), ms.at[i, c], mr.at[v, c]))
-        out.append(((g + 1) * views, g < bands - 1, low_edge, los.at[c], lor.at[v, c]))
-        out.append((g * views - 1, g > 0, high_edge, his.at[c], hir.at[v, c]))
+            out.append((in_band[i], seats[i], z >= 0, piece(i), ms.at[i, c], mr.at[v, c]))
+        out.append((band_sides[0], seats[views], g < bands - 1, low_edge, los.at[c], lor.at[v, c]))
+        out.append((band_sides[1], seats[views + 1], g > 0, high_edge, his.at[c], hir.at[v, c]))
         return out
 
     def join(c):
@@ -288,12 +296,12 @@
             follow = jnp.where(last_col, total, pltpu.roll(total, 127, 1))
             total = (1.0 - fx) * total + fx * follow
             joined_ref[0, p] = jnp.maximum(total / (covered + 1.0), DATA_FLOOR)
-        for target, ok, rows_of, send, recv in sends(c):
+        for target, seat, ok, rows_of, send, recv in sends(c):
             (lo, hi), (dlo, dhi) = rows_of
 
             @pl.when(ok & (target != me))
-            def _(rows_of=rows_of, target=target, send=send, recv=recv):
-                part_copy(c, v, rows_of, target, send, recv).start()
+            def _(rows_of=rows_of, seat=seat, send=send, recv=recv):
+                part_copy(c, v, rows_of, seat, send, recv).start()
 
             @pl.when(ok & (target == me))
             def _(lo=lo, hi=hi, dlo=dlo, dhi=dhi):
@@ -326,15 +334,15 @@
             for i in range(views):
                 @pl.when((idx == i) & ((w != v) | (band != g)))
                 def _(i=i, w=w):
-                    part_copy(c, w, piece(i), me, ms.at[i, c], mr.at[w, c]).wait_recv()
+                    part_copy(c, w, piece(i), (v, g), ms.at[i, c], mr.at[w, c]).wait_recv()
 
             @pl.when((idx == 0) & (band > 0) & ((w != v) | (band - 1 != g)))
             def _(w=w):
-                part_copy(c, w, low_edge, me, los.at[c], lor.at[w, c]).wait_recv()
+                part_copy(c, w, low_edge, (v, g), los.at[c], lor.at[w, c]).wait_recv()
 
             @pl.when((idx == views - 1) & (band < bands - 1) & ((w != v) | (band + 1 != g)))
             def _(w=w):
-                part_copy(c, w, high_edge, me, his.at[c], hir.at[w, c]).wait_recv()
+                part_copy(c, w, high_edge, (v, g), his.at[c], hir.at[w, c]).wait_recv()
 
         for p in range(c * CP, (c + 1) * CP):
             average(CZ + p)
@@ -373,13 +381,14 @@
         at = axis * taps + t
         return tap_all[w, at : at + 1, :]
 
-    def blur_rows(est, first):
-        for p in range(OC):
+    def blur_rows(est, first, size):
+        for p in range(size):
             terms = [est[first + p, t : t + rows_r, :] for t in range(taps)]
             for w in range(views):
                 zb[w, p] = weighted(terms, [tap(w, 1, t) for t in range(taps)])
         for w in range(views):
-            xb[w, pl.ds(first, OC)] = along_x(zb[w].reshape(OC * rows_r, 128), w, 0).reshape(OC, rows_r, 128)
+            mixed = along_x(zb[w, 0:size].reshape(size * rows_r, 128), w, 0)
+            xb[w, pl.ds(first, size)] = mixed.reshape(size, rows_r, 128)
 
     def ratios(r, at, w, lo, hi):
         base = CZ - 2 * margin
@@ -395,55 +404,58 @@
 
     def correct(est, emit):
         for c in range(NOUT):
-            done = c * OC + 2 * margin if c > 0 else 0
-            stop = (c + 1) * OC + 2 * margin
+            low, high = CUTS[c], CUTS[c + 1]
+            size = high - low
+            done = low + 2 * margin if c > 0 else 0
+            stop = high + 2 * margin
 
             @pl.loop(0, rows_r // 8, unroll=True)
-            def _(r, c=c, done=done, stop=stop):
+            def _(r, low=low, high=high, done=done, stop=stop):
                 at = pl.ds(pl.multiple_of(r * 8, 8), 8)
                 for w in range(views):
-                    ratio = [rt[w, p, at, :] for p in range(c * OC, done)] + ratios(r, at, w, done, stop)
-                    if c < NOUT - 1:
-                        for p in range((c + 1) * OC, stop):
-                            if p >= done:
-                                rt[w, p, at, :] = ratio[p - c * OC]
-                    for p in range(OC):
+                    ratio = [rt[w, p, at, :] for p in range(low, done)] + ratios(r, at, w, done, stop)
+                    if high < CZ:
+                        for p in range(max(high, done), stop):
+                            rt[w, p, at, :] = ratio[p - low]
+                    for p in range(high - low):
                         za[w, p, at, :] = weighted(ratio[p : p + taps], [tap(w, 0, taps - 1 - t) for t in range(taps)])
 
             factors = []
             for w in range(views):
-                for p in range(OC):
+                for p in range(size):
                     yb[w, p] = weighted([za[w, p, t : t + strip, :] for t in range(taps)],
                                         [tap(w, 1, taps - 1 - t) for t in range(taps)])
-                factors.append(along_x(yb[w].reshape(OC * strip, 128), w, 1).reshape(OC, strip, 128))
-            emit(c, est[pl.ds(CZ + c * OC, OC), HALO : HALO + strip, :] * root(factors))
+                factors.append(along_x(yb[w, 0:size].reshape(size * strip, 128), w, 1).reshape(size, strip, 128))
+            emit(c, est[pl.ds(CZ + low, size), HALO : HALO + strip, :] * root(factors))
+
+    def cut(c):
+        return pl.ds(CUTS[c], CUTS[c + 1] - CUTS[c])
 
     join(0)
     for c in range(1, NCH):
         join(c)
         spread(c - 1)
-    for c in range(NOUT - 1):
-        blur_rows(e0, CZ + c * OC)
+    for c in range(0, NCH - 1):
+        blur_rows(e0, CZ + c * CP, CP)
     spread(NCH - 1)
-    blur_rows(e0, 2 * CZ - OC)
-
-    for group in range(NOUT):
+    blur_rows(e0, 2 * CZ - CP, CP)
+
+    for c in range(NCH):
         for up, ok in ((True, below), (False, above)):
             @pl.when(ok)
-            def _(up=up, group=group):
-                for c in range(group * OC // CP, (group + 1) * OC // CP):
-                    copies = z_copies(c, up)
-                    for copy in copies:
-                        copy.wait_recv()
-                    if len(copies) == views and views > 1:
-                        for p in range(c * CP, (c + 1) * CP):
-                            average((0 if up else 2 * CZ) + p)
-
-            blur_rows(e0, (0 if up else 2 * CZ) + group * OC)
+            def _(up=up, c=c):
+                copies = z_copies(c, up)
+                for copy in copies:
+                    copy.wait_recv()
+                if len(copies) == views and views > 1:
+                    for p in range(c * CP, (c + 1) * CP):
+                        average((0 if up else 2 * CZ) + p)
+
+            blur_rows(e0, (0 if up else 2 * CZ) + c * CP, CP)
 
     inner = pl.ds(HALO, strip)
     near = []
-    for n, (dz, ds) in enumerate([(a, b) for a in (-1, 1, 0) for b in (0, -1, 1) if a or b]):
+    for n, (dz, ds) in enumerate([(a, b) for b in (-1, 1) for a in (-1, 1)] + [(-1, 0), (1, 0), (0, -1), (0, 1)]):
         zok = {-1: below, 0: z >= 0, 1: above}[dz]
         sok = {-1: left, 0: z >= 0, 1: right}[ds]
         far_z = {-1: above, 0: z >= 0, 1: below}[dz]
@@ -453,13 +465,14 @@
     def near_copy(n, dz, ds, c):
         src_r = {-1: pl.ds(HALO, HALO), 0: inner, 1: pl.ds(strip, HALO)}[ds]
         dst_r = {-1: pl.ds(HALO + strip, HALO), 0: inner, 1: pl.ds(0, HALO)}[ds]
-        dst = {-1: 2 * CZ, 0: CZ, 1: 0}[dz] + c * OC
+        dst = CZ - dz * CZ + CUTS[c]
+        size = CUTS[c + 1] - CUTS[c]
         return pltpu.make_async_remote_copy(
-            src_ref=e1.at[pl.ds(CZ + c * OC, OC), src_r, :], dst_ref=e1.at[pl.ds(dst, OC), dst_r, :],
-            send_sem=es.at[n, c], recv_sem=er.at[n, c], device_id=strip_dev(z + dz, me + ds), device_id_type=MESH)
+            src_ref=e1.at[pl.ds(CZ + CUTS[c], size), src_r, :], dst_ref=e1.at[pl.ds(dst, size), dst_r, :],
+            send_sem=es.at[n, c], recv_sem=er.at[n, c], device_id=dev(z + dz, *around[ds]), device_id_type=MESH)
 
     def emit_step(c, new):
-        e1[pl.ds(CZ + c * OC, OC), HALO : HALO + strip, :] = new
+        e1[pl.ds(CZ + CUTS[c], CUTS[c + 1] - CUTS[c]), HALO : HALO + strip, :] = new
         for n, dz, ds, ok, _ in near:
             @pl.when(ok)
             def _(n=n, dz=dz, ds=ds):
@@ -479,10 +492,10 @@
                 down_copy(acc_ref, t, c).wait_send()
 
     for c in range(NCH):
-        for target, ok, rows_of, send, recv in sends(c):
+        for target, seat, ok, rows_of, send, recv in sends(c):
             @pl.when(ok & (target != me))
-            def _(rows_of=rows_of, target=target, send=send, recv=recv, c=c):
-                part_copy(c, v, rows_of, target, send, recv).wait_send()
+            def _(rows_of=rows_of, seat=seat, send=send, recv=recv, c=c):
+                part_copy(c, v, rows_of, seat, send, recv).wait_send()
 
         for up, ok in ((True, above), (False, below)):
             @pl.when(ok)
@@ -499,21 +512,21 @@
 
     for c in range(NOUT):
         near_wait(c, 0)
-        blur_rows(e1, CZ + c * OC)
+        blur_rows(e1, CZ + CUTS[c], CUTS[c + 1] - CUTS[c])
     for c in range(NOUT):
         for way in (1, -1):
             near_wait(c, way)
-            blur_rows(e1, CZ - way * CZ + c * OC)
+            blur_rows(e1, CZ - way * CZ + CUTS[c], CUTS[c + 1] - CUTS[c])
 
     def out_copy(c, w, target_g, i):
         at = pl.ds(pl.multiple_of(i * strip, 8), strip)
-        part = pl.ds(c * OC, OC)
+        part = cut(c)
         return pltpu.make_async_remote_copy(
             src_ref=lg.at[part], dst_ref=est_ref.at[part, at, :], send_sem=out_s.at[w, c],
             recv_sem=out_r.at[i, c], device_id=dev(z, w, target_g), device_id_type=MESH)
 
     def emit_last(c, new):
-        lg[pl.ds(c * OC, OC)] = new
+        lg[cut(c)] = new
         for w in range(views):
             away = (w != v) | (band != g)
 
@@ -523,7 +536,7 @@
 
             @pl.when(jnp.logical_not(away))
             def _():
-                est_ref[pl.ds(c * OC, OC), pl.ds(pl.multiple_of(idx * strip, 8), strip), :] = new
+                est_ref[cut(c), pl.ds(pl.multiple_of(idx * strip, 8), strip), :] = new
 
     correct(e1, emit_last)
 
@@ -597,8 +610,8 @@
     ]
     late = [
         (views, 3 * CZ, strip + 2 * margin, cols), (views, CZ + 2 * margin, strip + 2 * margin, cols),
-        (views, OC, strip + 2 * margin, cols),
-        (views, OC, strip + 2 * margin, cols), (views, OC, strip, cols), (CZ, strip, cols),
+        (views, MOST, strip + 2 * margin, cols),
+        (views, MOST, strip + 2 * margin, cols), (views, MOST, strip, cols), (CZ, strip, cols),
     ]
     total = sum([functools.reduce(lambda a, b: a * b, s) for s in shapes + late])
     total = total + cols * (slabs * tall + 2 * CZ * rows + views * 4 * cols)

time: 48.8 us -> 48.3 us (0.990); the launches traced: 48.6 us -> 47.3 us
  Pallas kernels: 47.3 us -> 46 us
    pallas_call x1, Pallas kernels: 44.5 us -> 43.2 us  [on_device(): pl.pallas_call(functools.partial(world_kernel, dims, rows, taps), in_spec...]
where the time goes in v8:
time: 48.3 us; the launch traced here: 47.3 us
  Pallas kernels  46 us (95%)
  between operations  1.29 us (3%)
    pallas_call x1, Pallas kernels, on_device(): pl.pallas_call(functools.partial(world_kernel, dims, rows, taps), in_spec...  43.2 us
    pallas_call x1, Pallas kernels, on_device(): pl.pallas_call(functools.partial(deposit_kernel, rows), in_specs=[any_hbm...  1.99 us

profile of v8, /device:TPU:1, one launch (start us, length us, event | category | flops | bytes accessed | tf_op | source)
XLA Modules:
  0.0 47.3 jit_solution(3572672746143872144)
XLA Ops:
  1.3 2.0 %deposit.1.acc_ref = f32[4,520,128]{2,1,0:T(8,128)S(1)} custom-call(s32[32]{0:T(128)} %bitcast.9, s32[32]{0:T(128)} %bitcast.10, s32[1,1,1]{2,1,0:T(1,128)S(6)} %copy.8.level_in, f32[3]{0:T(128)} %bitcast.6, f32[32,3,64,128]{3,2,1,0:T(8,128)} %bitcast.5), custom_call_target="tpu_custom_call" | custom-call | tf_op jit(solution)/shard_map/deposit/pallas_call | solution.py:585
  3.3 43.2 %world.1 = (f32[8,64,128]{2,1,0:T(8,128)S(1)}, f32[1,8,64,128]{3,2,1,0:T(8,128)S(1)}) custom-call(f32[4,520,128]{2,1,0:T(8,128)S(1)} %deposit.1.acc_ref, f32[3]{0:T(128)} %bitcast.7, f32[3,1,9]{2,1,0:T(1,128)} %bitcast.8), custom_call_target="tpu_custom_call" | custom-call | tf_op jit(solution)/shard_map/world/pallas_call | solution.py:618
  46.5 0.8 %store.1 = (f32[8,64,128]{2,1,0:T(8,128)}, f32[1,8,64,128]{3,2,1,0:T(8,128)}) custom-call(f32[8,64,128]{2,1,0:T(8,128)S(1)} %get-tuple-element.4.est_in, f32[1,8,64,128]{3,2,1,0:T(8,128)S(1)} %get-tuple-element.5.joined_in), custom_call_target="tpu_custom_call" | custom-call | tf_op jit(solution)/shard_map/store/pallas_call | solution.py:641

commit v9 on v8

--- a/solution.py
+++ b/solution.py
@@ -346,7 +346,7 @@
 
         for p in range(c * CP, (c + 1) * CP):
             average(CZ + p)
-        for up, ok in ((True, above), (False, below)):
+        for up, ok in ((False, below), (True, above)):
             @pl.when(ok)
             def _(up=up):
                 for copy in z_copies(c, up):

time: 48.3 us -> 48.3 us (level)
  no operation moved by 1% of the time
where the time goes in v9:
time: 48.3 us; the launch traced here: 47.3 us
  Pallas kernels  46 us (95%)
  between operations  1.29 us (3%)
    pallas_call x1, Pallas kernels, on_device(): pl.pallas_call(functools.partial(world_kernel, dims, rows, taps), in_spec...  43.2 us
    pallas_call x1, Pallas kernels, on_device(): pl.pallas_call(functools.partial(deposit_kernel, rows), in_specs=[any_hbm...  1.99 us

profile of v9, /device:TPU:1, one launch (start us, length us, event | category | flops | bytes accessed | tf_op | source)
XLA Modules:
  0.0 47.3 jit_solution(11542966682983697633)
XLA Ops:
  1.3 2.0 %deposit.1.acc_ref = f32[4,520,128]{2,1,0:T(8,128)S(1)} custom-call(s32[32]{0:T(128)} %bitcast.9, s32[32]{0:T(128)} %bitcast.10, s32[1,1,1]{2,1,0:T(1,128)S(6)} %copy.8.level_in, f32[3]{0:T(128)} %bitcast.6, f32[32,3,64,128]{3,2,1,0:T(8,128)} %bitcast.5), custom_call_target="tpu_custom_call" | custom-call | tf_op jit(solution)/shard_map/deposit/pallas_call | solution.py:585
  3.3 43.2 %world.1 = (f32[8,64,128]{2,1,0:T(8,128)S(1)}, f32[1,8,64,128]{3,2,1,0:T(8,128)S(1)}) custom-call(f32[4,520,128]{2,1,0:T(8,128)S(1)} %deposit.1.acc_ref, f32[3]{0:T(128)} %bitcast.7, f32[3,1,9]{2,1,0:T(1,128)} %bitcast.8), custom_call_target="tpu_custom_call" | custom-call | tf_op jit(solution)/shard_map/world/pallas_call | solution.py:618
  46.5 0.8 %store.1 = (f32[8,64,128]{2,1,0:T(8,128)}, f32[1,8,64,128]{3,2,1,0:T(8,128)}) custom-call(f32[8,64,128]{2,1,0:T(8,128)S(1)} %get-tuple-element.4.est_in, f32[1,8,64,128]{3,2,1,0:T(8,128)S(1)} %get-tuple-element.5.joined_in), custom_call_target="tpu_custom_call" | custom-call | tf_op jit(solution)/shard_map/store/pallas_call | solution.py:641
